TPU v7x, 512 devices: a whole 4x4x16 slice. The times are simulated.
512 devices in a mesh: lat: 64 (over z, y), mem: 8 (over x, core).
Axes of the slice: x: 4, y: 4, z: 16, core: 2. Of those that a mesh axis runs over, the one named last changes fastest.
Arguments:
- ens_perts: bfloat16 [8, 64, 384, 768], P('mem', None, 'lat'), may hold values from -6 to 6
- vert_loc: float32 [64, 64], replicated, may hold values from 0 to 1.8
- lat_lengths: float32 [3], replicated, may hold values from 1.5 to 32
- lon_lengths: float32 [3], replicated, may hold values from 1.5 to 1.7
- scale_weights: float32 [3], replicated, may hold values from 0.3 to 1
- obs_cell: int32 [524288], P('lat'), may hold values from 0 to 294911
- obs_accept: int32 [524288], P('lat'), may hold values 0 or 1
- innovation: float32 [524288], P('lat'), may hold values from -6 to 6
- obs_precision: float32 [524288], P('lat'), may hold values from 0.25 to 4
Outputs:
- new_control: float32 [8, 64, 384, 768], P('mem', None, 'lat')
- gradient: float32 [8, 64, 384, 768], P('mem', None, 'lat')
Inputs may be any that keep to these rules, and one draw needn't show every extreme that they name: `obs_cell`: an observation's cell lies in the band of the device that holds it. `obs_accept`: 1 accepts the observation, 0 rejects it.
All inputs are finite; a program needn't handle non-finite values. No bound on the sum of `obs_accept` on one device may be relied on, other than what follows from the above.
Results may differ from a plain program's by a relative error of at most 0.009.
Values may be sent and summed in bfloat16 or wider, within the bound.
A program may use at most 64 MiB of HBM per device.

v0:
```python
import functools

import jax
import jax.numpy as jnp
from jax import lax
from jax.sharding import Mesh
from jax.sharding import PartitionSpec as P

LAT = ("lat_0", "lat_1")
MEM = ("mem_0", "mem_1")
LAT_MEM = ("lat_0", "lat_1", "mem_0", "mem_1")


def sent_to_all(array, axis):
    copies = jnp.broadcast_to(array, (lax.axis_size(axis), *array.shape))
    return lax.all_to_all(copies, axis, split_axis=0, concat_axis=0, tiled=True)


def of_everyone(array, axis):
    everything = sent_to_all(array, axis)
    return jnp.sum(everything.astype(jnp.float32), axis=0)


def one_axis_at_a_time(array, axes):
    return functools.reduce(lax.psum, axes, array)


def gaussian_table(lengths, count, periodic):
    positions = jnp.arange(count, dtype=jnp.float32)
    distance = jnp.abs(positions[:, None] - positions[None, :])
    if periodic:
        distance = jnp.minimum(distance, count - distance)
    scaled = distance[None] / lengths[:, None, None]
    return jnp.exp(-0.5 * scaled * scaled).astype(jnp.bfloat16)


def correlate(level_field, tables):
    lat_corr, lon_corr, scale_weights = tables
    summed = jnp.zeros(level_field.shape, jnp.float32)
    for scale_index in range(lat_corr.shape[0]):
        across = jnp.einsum(
            "ab,mlbc->mlac", lat_corr[scale_index], level_field, preferred_element_type=jnp.float32
        ).astype(jnp.bfloat16)
        summed = summed + scale_weights[scale_index] * jnp.einsum(
            "mlac,cd->mlad", across, lon_corr[scale_index], preferred_element_type=jnp.float32
        )
    return summed.astype(jnp.bfloat16)


def vertical(matrix, values):
    return jnp.einsum("ij,mjrc->mirc", matrix, values, precision=lax.Precision.HIGHEST)


def vertical_adjoint(matrix, values):
    return jnp.einsum("ji,mjrc->mirc", matrix, values, precision=lax.Precision.HIGHEST)


def band_correlate(band_field, tables):
    owned = correlate(
        lax.all_to_all(band_field, LAT, split_axis=1, concat_axis=2, tiled=True), tables=tables
    )
    return lax.all_to_all(owned, LAT, split_axis=2, concat_axis=1, tiled=True)


def local(
    ens_perts,
    vert_loc,
    lat_lengths,
    lon_lengths,
    scale_weights,
    obs_cell,
    obs_accept,
    innovation,
    obs_precision,
):
    members, levels, band_rows, lon_count = ens_perts.shape
    band_count = lax.axis_size(LAT)
    height = band_rows * band_count
    tables = (
        gaussian_table(lat_lengths, height, False),
        gaussian_table(lon_lengths, lon_count, True),
        scale_weights,
    )
    obs_weight = obs_accept.astype(jnp.float32) * obs_precision
    cell_count = levels * band_rows * lon_count
    pert_at_obs = ens_perts.reshape(members, cell_count)[:, obs_cell].astype(jnp.float32)

    def adjoint(obs_values):
        spread = (
            jnp.zeros((cell_count,), jnp.float32)
            .at[obs_cell]
            .add(obs_values)
            .reshape(levels, band_rows, lon_count)
        )
        schur = (ens_perts.astype(jnp.float32) * spread[None]).astype(jnp.bfloat16)
        corr_back = band_correlate(schur, tables)
        return vertical_adjoint(vert_loc, corr_back.astype(jnp.float32))

    first_grad = -adjoint(obs_weight * innovation)
    grad_local = jnp.sum(first_grad * first_grad)
    localized = vertical(vert_loc, first_grad).astype(jnp.bfloat16)
    corr = band_correlate(localized, tables)
    corr_at_obs = corr.reshape(members, cell_count)[:, obs_cell].astype(jnp.float32)
    partial_obs = jnp.sum(pert_at_obs * corr_at_obs, axis=0)
    first_image = of_everyone(partial_obs.astype(jnp.bfloat16), MEM).astype(jnp.float32)
    obs_local = jnp.where(
        lax.axis_index(MEM) == 0, jnp.sum(obs_weight * first_image * first_image), 0.0
    )
    grad_square, obs_square = (
        one_axis_at_a_time(grad_local, LAT_MEM),
        one_axis_at_a_time(obs_local, LAT_MEM),
    )
    first_step = grad_square / (grad_square + obs_square)
    first_control = -first_step * first_grad
    misfit = -first_step * first_image - innovation
    gradient = first_control + adjoint(obs_weight * misfit)
    change = gradient - first_grad
    cross_sum, change_sum = (
        one_axis_at_a_time(jnp.sum(first_control * change), LAT_MEM),
        one_axis_at_a_time(jnp.sum(change * change), LAT_MEM),
    )
    new_control = first_control - cross_sum / change_sum * gradient
    return (new_control, gradient)


def solution(mesh):
    split = Mesh(mesh.devices.reshape(16, 4, 4, 2), ("lat_0", "lat_1", "mem_0", "mem_1"))
    placed = (P(MEM, None, LAT, None), P(), P(), P(), P(), P(LAT), P(LAT), P(LAT), P(LAT))
    return jax.shard_map(
        local,
        mesh=split,
        in_specs=placed,
        out_specs=(P(MEM, None, LAT, None), P(MEM, None, LAT, None)),
        check_vma=False,
    )
```

profile of v0, /device:TPU:1, one launch (start us, length us, event | category | flops | bytes accessed | tf_op | source)
XLA Modules:
  0.0 657.2 jit_solution(13395269953196016115)
XLA Ops:
  2.2 43.5 %scatter_custom_fusion = f32[294912]{0:T(1024)S(1)} fusion(s32[8192]{0:T(1024)S(1)} %get-tuple-element.21, f32[8192]{0:T(1024)S(1)} %fusion.44, f32[]{:T(128)} %constant.8.clone.1), kind=kCustom, calls=%fused_computation.77 | custom fusion | flops 8192 | bytes 1179652 | tf_op jit(solution)/shard_map/scatter-add | solution.py:92
  48.1 19.6 %all-to-all-start = ((bf16[1,64,6,768]{3,2,0,1:T(8,128)(2,1)}), bf16[1,64,6,768]{3,2,0,1:T(8,128)(2,1)S(1)}, u32[]{:S(2)}, u32[]{:S(2)}) async-start(bf16[1,64,6,768]{3,2,0,1:T(8,128)(2,1)} %fusion.32), calls=%async_computation | async-start | bytes 1572864 | tf_op jit(solution)/shard_map/all_to_all | solution.py:60
  72.8 35.6 %all-to-all-done = bf16[1,64,6,768]{3,2,0,1:T(8,128)(2,1)S(1)} async-done(((bf16[1,64,6,768]{3,2,0,1:T(8,128)(2,1)}), bf16[1,64,6,768]{3,2,0,1:T(8,128)(2,1)S(1)}, u32[]{:S(2)}, u32[]{:S(2)}) %all-to-all-start) | async-done | bytes 589856 | tf_op jit(solution)/shard_map/all_to_all | solution.py:60
  126.0 40.3 %all_to_all.29 = bf16[64,2,2304]{2,1,0:T(2,128)(2,1)S(1)} all-to-all(bf16[64,2,2304]{2,1,0:T(2,128)(2,1)S(1)} %reshape.263), channel_id=1, replica_groups=mesh['lat_0'=16,'lat_1'=4,'mem_0'=4,'mem_1'=2] {'lat_0','lat_1'}, dimensions={0} | all-to-all | bytes 1179648 | tf_op jit(solution)/shard_map/all_to_all | solution.py:62
  173.5 48.6 %all_to_all.30 = bf16[1,64,6,768]{3,2,0,1:T(8,128)(2,1)S(1)} all-to-all(bf16[1,64,6,768]{3,2,0,1:T(8,128)(2,1)S(1)} %copy.77), channel_id=1, replica_groups=mesh['lat_0'=16,'lat_1'=4,'mem_0'=4,'mem_1'=2] {'lat_0','lat_1'}, dimensions={1} | all-to-all | bytes 1179648 | tf_op jit(solution)/shard_map/all_to_all | solution.py:60
  227.7 4.7 fusion.9
  238.8 4.9 reduce.10
  246.4 9.2 %all-to-all-start.3 = ((bf16[64,2,2304]{2,1,0:T(2,128)(2,1)}), bf16[64,2,2304]{2,1,0:T(2,128)(2,1)S(1)}, u32[]{:S(2)}, u32[]{:S(2)}) async-start(bf16[64,2,2304]{2,1,0:T(2,128)(2,1)} %reshape.265), calls=%async_computation.3 | async-start | bytes 1179648 | tf_op jit(solution)/shard_map/all_to_all | solution.py:62
  256.5 50.7 %gather_fusion = bf16[8192]{0:T(1024)(128)(2,1)S(1)} fusion(bf16[294912]{0:T(1024)(128)(2,1)S(1)} %reshape.206, s32[8192]{0:T(1024)S(1)} %get-tuple-element.20), kind=kCustom, calls=%fused_computation | custom fusion | bytes 65536 | tf_op jit(solution)/shard_map/gather | solution.py:86
  311.7 50.7 %gather_fusion.1 = bf16[8192]{0:T(1024)(128)(2,1)S(1)} fusion(bf16[294912]{0:T(1024)(128)(2,1)S(1)} %reshape.216, s32[8192]{0:T(1024)S(1)} %get-tuple-element.20), kind=kCustom, calls=%fused_computation.1 | custom fusion | bytes 65536 | tf_op jit(solution)/shard_map/gather | solution.py:103
  364.7 6.7 %all-to-all-start.4 = ((bf16[8,2,4096]{2,1,0:T(2,128)(2,1)}), bf16[8,2,4096]{2,1,0:T(2,128)(2,1)S(1)}, u32[]{:S(2)}, u32[]{:S(2)}) async-start(bf16[8,2,4096]{2,1,0:T(2,128)(2,1)} %reshape.267), calls=%async_computation.4 | async-start | bytes 262144 | tf_op jit(solution)/shard_map/all_to_all | solution.py:16
  371.4 5.2 all-to-all-done.4
  378.2 24.2 %all-reduce.1 = (f32[]{:T(128)}, f32[]{:T(128)}) all-reduce(f32[]{:T(128)} %get-tuple-element.25, f32[]{:T(128)S(6)} %select_n.11), channel_id=1, replica_groups=mesh['lat_0'=16,'lat_1'=4,'mem_0'=4,'mem_1'=2] {'lat_0'}, use_global_device_ids=true, to_apply=%region_2.0 | all-reduce | flops 2 | bytes 16 | tf_op jit(solution)/shard_map/psum | solution.py:25
  402.5 9.0 %all-reduce.5 = (f32[]{:T(128)}, f32[]{:T(128)}) all-reduce(f32[]{:T(128)} %get-tuple-element.6, f32[]{:T(128)} %get-tuple-element.7), channel_id=1, replica_groups=mesh['lat_0'=16,'lat_1'=4,'mem_0'=4,'mem_1'=2] {'lat_1'}, use_global_device_ids=true, to_apply=%region_3.0 | all-reduce | flops 2 | bytes 16 | tf_op jit(solution)/shard_map/psum | solution.py:25
  411.5 7.5 %all-reduce.3 = (f32[]{:T(128)}, f32[]{:T(128)}) all-reduce(f32[]{:T(128)} %get-tuple-element.14, f32[]{:T(128)} %get-tuple-element.15), channel_id=1, replica_groups=mesh['lat_0'=16,'lat_1'=4,'mem_0'=4,'mem_1'=2] {'mem_0'}, use_global_device_ids=true, to_apply=%region_4.0 | all-reduce | flops 2 | bytes 16 | tf_op jit(solution)/shard_map/psum | solution.py:25
  419.0 14.6 %all-reduce.7 = (f32[]{:T(128)}, f32[]{:T(128)}) all-reduce(f32[]{:T(128)} %get-tuple-element.10, f32[]{:T(128)} %get-tuple-element.11), channel_id=1, replica_groups=mesh['lat_0'=16,'lat_1'=4,'mem_0'=4,'mem_1'=2] {'mem_1'}, use_global_device_ids=true, to_apply=%region_5.6 | all-reduce | flops 2 | bytes 16 | tf_op jit(solution)/shard_map/psum | solution.py:25
  435.5 44.2 %scatter_custom_fusion.1 = f32[294912]{0:T(1024)} fusion(s32[8192]{0:T(1024)S(1)} %get-tuple-element.21, f32[8192]{0:T(1024)S(1)} %subtract_multiply_fusion, f32[]{:T(128)} %constant.8.clone.1), kind=kCustom, calls=%fused_computation.75 | custom fusion | flops 8192 | bytes 1179652 | tf_op jit(solution)/shard_map/scatter-add | solution.py:92
  481.7 51.0 %all_to_all.62 = bf16[1,64,6,768]{3,2,0,1:T(8,128)(2,1)S(1)} all-to-all(bf16[1,64,6,768]{3,2,0,1:T(8,128)(2,1)S(1)} %fusion.31), channel_id=1, replica_groups=mesh['lat_0'=16,'lat_1'=4,'mem_0'=4,'mem_1'=2] {'lat_0','lat_1'}, dimensions={1} | all-to-all | bytes 1179648 | tf_op jit(solution)/shard_map/all_to_all | solution.py:60
  537.2 4.7 fusion.7
  551.1 40.4 %all_to_all.63 = bf16[64,2,2304]{2,1,0:T(2,128)(2,1)S(1)} all-to-all(bf16[64,2,2304]{2,1,0:T(2,128)(2,1)S(1)} %reshape.269), channel_id=1, replica_groups=mesh['lat_0'=16,'lat_1'=4,'mem_0'=4,'mem_1'=2] {'lat_0','lat_1'}, dimensions={0} | all-to-all | bytes 1179648 | tf_op jit(solution)/shard_map/all_to_all | solution.py:62
  599.1 23.3 %all-reduce = (f32[]{:T(128)}, f32[]{:T(128)}) all-reduce(f32[]{:T(128)} %get-tuple-element.3, f32[]{:T(128)} %get-tuple-element.2), channel_id=1, replica_groups=mesh['lat_0'=16,'lat_1'=4,'mem_0'=4,'mem_1'=2] {'lat_0'}, use_global_device_ids=true, to_apply=%region_14.15 | all-reduce | flops 2 | bytes 16 | tf_op jit(solution)/shard_map/psum | solution.py:25
  622.4 9.7 %all-reduce.4 = (f32[]{:T(128)}, f32[]{:T(128)}) all-reduce(f32[]{:T(128)} %get-tuple-element.4, f32[]{:T(128)} %get-tuple-element.5), channel_id=1, replica_groups=mesh['lat_0'=16,'lat_1'=4,'mem_0'=4,'mem_1'=2] {'lat_1'}, use_global_device_ids=true, to_apply=%region_15.16 | all-reduce | flops 2 | bytes 16 | tf_op jit(solution)/shard_map/psum | solution.py:25
  632.1 7.2 %all-reduce.2 = (f32[]{:T(128)}, f32[]{:T(128)}) all-reduce(f32[]{:T(128)} %get-tuple-element.12, f32[]{:T(128)} %get-tuple-element.13), channel_id=1, replica_groups=mesh['lat_0'=16,'lat_1'=4,'mem_0'=4,'mem_1'=2] {'mem_0'}, use_global_device_ids=true, to_apply=%region_16.17 | all-reduce | flops 2 | bytes 16 | tf_op jit(solution)/shard_map/psum | solution.py:25
  639.3 15.2 %all-reduce.6 = (f32[]{:T(128)}, f32[]{:T(128)}) all-reduce(f32[]{:T(128)} %get-tuple-element.8, f32[]{:T(128)} %get-tuple-element.9), channel_id=1, replica_groups=mesh['lat_0'=16,'lat_1'=4,'mem_0'=4,'mem_1'=2] {'mem_1'}, use_global_device_ids=true, to_apply=%region_17.18 | all-reduce | flops 2 | bytes 16 | tf_op jit(solution)/shard_map/psum | solution.py:25
  (87 shorter events, 81.4 us)
Async XLA Ops:
  0.6 169.9 %copy-start = (f32[64,64]{1,0:T(8,128)S(1)}, f32[64,64]{1,0:T(8,128)}, u32[]{:S(2)}) copy-start(f32[64,64]{1,0:T(8,128)} %param.10) | copy-start | bytes 49156
  45.7 1.1 copy-start.1
  48.1 19.6 %copy-start.13 = (f32[3]{0:T(128)S(1)}, f32[3]{0:T(128)}, u32[]{:S(2)}) copy-start(f32[3]{0:T(128)} %param.13) | copy-start | bytes 40
  48.1 60.4 %all-to-all-start = ((bf16[1,64,6,768]{3,2,0,1:T(8,128)(2,1)}), bf16[1,64,6,768]{3,2,0,1:T(8,128)(2,1)S(1)}, u32[]{:S(2)}, u32[]{:S(2)}) async-start(bf16[1,64,6,768]{3,2,0,1:T(8,128)(2,1)} %fusion.32), calls=%async_computation | async-start | bytes 1572864 | tf_op jit(solution)/shard_map/all_to_all | solution.py:60
  68.4 0.7 copy-start.14
  69.0 0.7 copy-start.15
  69.7 47.0 %copy-start.4 = (bf16[3,384,384]{2,1,0:T(8,128)(2,1)}, bf16[3,384,384]{2,1,0:T(8,128)(2,1)S(1)}, u32[]{:S(2)}) copy-start(bf16[3,384,384]{2,1,0:T(8,128)(2,1)S(1)} %fusion.3) | copy-start | bytes 2654212
  108.6 4.4 copy-start.8
  173.5 49.6 %copy-start.5 = (bf16[3,384,384]{2,1,0:T(8,128)(2,1)S(1)}, bf16[3,384,384]{2,1,0:T(8,128)(2,1)}, u32[]{:S(2)}) copy-start(bf16[3,384,384]{2,1,0:T(8,128)(2,1)} %copy-done.4) | copy-start | bytes 2654212
  223.1 4.6 copy-start.9
  246.4 60.8 %all-to-all-start.3 = ((bf16[64,2,2304]{2,1,0:T(2,128)(2,1)}), bf16[64,2,2304]{2,1,0:T(2,128)(2,1)S(1)}, u32[]{:S(2)}, u32[]{:S(2)}) async-start(bf16[64,2,2304]{2,1,0:T(2,128)(2,1)} %reshape.265), calls=%async_computation.3 | async-start | bytes 1179648 | tf_op jit(solution)/shard_map/all_to_all | solution.py:62
  362.4 14.5 %copy-start.10 = (f32[8192]{0:T(1024)S(1)}, f32[8192]{0:T(1024)}, u32[]{:S(2)}) copy-start(f32[8192]{0:T(1024)} %param.17) | copy-start | bytes 98308
  362.5 14.5 %copy-start.11 = (s32[8192]{0:T(1024)S(1)}, s32[8192]{0:T(1024)}, u32[]{:S(2)}) copy-start(s32[8192]{0:T(1024)} %param.15) | copy-start | bytes 98308
  362.5 73.0 %copy-start.12 = (f32[8192]{0:T(1024)S(1)}, f32[8192]{0:T(1024)}, u32[]{:S(2)}) copy-start(f32[8192]{0:T(1024)} %param.16) | copy-start | bytes 98308
  364.7 11.9 %all-to-all-start.4 = ((bf16[8,2,4096]{2,1,0:T(2,128)(2,1)}), bf16[8,2,4096]{2,1,0:T(2,128)(2,1)S(1)}, u32[]{:S(2)}, u32[]{:S(2)}) async-start(bf16[8,2,4096]{2,1,0:T(2,128)(2,1)} %reshape.267), calls=%async_computation.4 | async-start | bytes 262144 | tf_op jit(solution)/shard_map/all_to_all | solution.py:16
  479.7 1.5 copy-start.2
  481.7 51.2 %copy-start.6 = (bf16[3,384,384]{2,1,0:T(8,128)(2,1)S(1)}, bf16[3,384,384]{2,1,0:T(8,128)(2,1)}, u32[]{:S(2)}) copy-start(bf16[3,384,384]{2,1,0:T(8,128)(2,1)} %copy-done.4) | copy-start | bytes 2654212
  532.9 4.4 copy-start.7
  599.1 57.9 %copy-start.3 = (f32[1,64,6,768]{3,1,2,0:T(8,128)}, f32[1,64,6,768]{3,1,2,0:T(8,128)S(1)}, u32[]{:S(2)}) copy-start(f32[1,64,6,768]{3,1,2,0:T(8,128)S(1)} %get-tuple-element.27) | copy-start | bytes 3538948
where the time goes:
time: 661 us; the launch traced here: 657 us
  blocking collectives  291 us (44%)
  local copies, waits for them, and re-layouts  131 us (20%)
  other arithmetic  112 us (17%)
  matrix products  42.3 us (6%)
  waiting for transfers between devices  40.9 us (6%)
  starting transfers between devices  35.4 us (5%)
    psum x8, blocking collectives, one_axis_at_a_time(): return functools.reduce(lax.psum, axes, array)  111 us
    all_to_all x2, blocking collectives, band_correlate(): lax.all_to_all(band_field, LAT, split_axis=1, concat_axis=2, tiled=True)  99.5 us
    scatter-add x2, other arithmetic, adjoint(): spread = jnp.zeros((cell_count,), jnp.float32).at[obs_cell].add(obs_value...  87.7 us
    all_to_all x2, blocking collectives, band_correlate(): return lax.all_to_all(owned, LAT, split_axis=2, concat_axis=1, tiled=True)  80.7 us
    gather x1, local copies, waits for them, and re-layouts, local(): corr.reshape(members, cell_count)[:, obs_cell].astype(jnp.float32)  50.7 us
    gather x1, local copies, waits for them, and re-layouts, local(): ens_perts.reshape(members, cell_count)[:, obs_cell].astype(jnp.float32)  50.7 us
    dot_general x9, matrix products, correlate(): jnp.einsum('mlac,cd->mlad', across, lon_corr[scale_index], preferred_elem...  38 us
    all_to_all x1, waiting for transfers between devices, band_correlate(): lax.all_to_all(band_field, LAT, split_axis=1, concat_axis=2, tiled=True)  35.6 us
  transfers between devices with their start and end apart: 3, of which 2 were waited for; matrix products, arithmetic and copies ran while one was open for 9% of the time, Pallas kernels for 0%

commit v1 on v0

v1 whole, which is shorter than its diff:
```python
import jax
import jax.numpy as jnp
from jax import lax
from jax.experimental import pallas as pl
from jax.experimental.pallas import tpu as pltpu
from jax.sharding import Mesh
from jax.sharding import PartitionSpec as P

LAT = ("lat_0", "lat_1")
MEM = ("mem_0", "mem_1")
MESH_ID = pl.DeviceIdType.MESH
NZ, NYC, NXC, NC = 16, 4, 4, 2
BANDS = NZ * NYC
MEMS = NXC * NC
LEV = 64
ROWS = 6
PAD = 8
NX = 768
LINES = ROWS * LEV
WIDE = LEV * PAD
SCALES = 3
OBS = 8192
CHUNK = 512
BF = jnp.bfloat16
F32 = jnp.float32

X1, UU, TT, X2, RR, RS, AG, SM, SL = range(9)


def iota(shape, dim):
    return lax.broadcasted_iota(jnp.int32, shape, dim)


def dot(a, b):
    return jnp.dot(a, b, preferred_element_type=F32)


def kernel(
    pert_ref,
    vert_ref,
    latlen_ref,
    lonlen_ref,
    sw_ref,
    cell_ref,
    accept_ref,
    innov_ref,
    prec_ref,
    f_ref,
    h_ref,
    sums_ref,
    perm,
    lat_tab,
    lon_tab,
    grad_mix,
    image_mix,
    line_ref,
    col_ref,
    field,
    weight,
    acc,
    across,
    flat,
    send_x,
    send_t,
    send_u,
    send_y,
    send_r,
    recv_x,
    recv_t,
    recv_u,
    recv_y,
    recv_r,
    part,
    part_in,
    own,
    image,
    row_mem,
    row_lat,
    sums_mem,
    sums_lat,
    send_sem,
    recv_sem,
):
    z = lax.axis_index("lat_0")
    y = lax.axis_index("lat_1")
    x = lax.axis_index("mem_0")
    c = lax.axis_index("mem_1")
    band = z * NYC + y
    mem = x * NC + c

    def lat_peer(k):
        j = k // NYC
        dz = NZ // 2 + ((j + 1) // 2) * (1 - 2 * (j % 2))
        zz = (z + dz) % NZ
        yy = (y + (NYC - 1) - k % NYC) % NYC
        return zz * NYC + yy, {"lat_0": zz, "lat_1": yy}

    def mem_peer(k):
        other = (mem + k) % MEMS
        return other, {"mem_0": other // NC, "mem_1": other % NC}

    barrier = pltpu.get_barrier_semaphore()

    def greet_lat(k, carry):
        pl.semaphore_signal(barrier, inc=1, device_id=lat_peer(k)[1], device_id_type=MESH_ID)
        return carry

    def greet_mem(k, carry):
        pl.semaphore_signal(barrier, inc=1, device_id=mem_peer(k)[1], device_id_type=MESH_ID)
        return carry

    lax.fori_loop(0, BANDS - 1, greet_lat, 0)
    lax.fori_loop(1, MEMS, greet_mem, 0)

    def remote(src, dst, phase, to):
        return pltpu.make_async_remote_copy(
            src_ref=src,
            dst_ref=dst,
            send_sem=send_sem.at[phase],
            recv_sem=recv_sem.at[phase],
            device_id=to,
            device_id_type=MESH_ID,
        )

    def lat_start(src, dst, phase):
        def go(k, carry):
            there, to = lat_peer(k)
            remote(src.at[there, pl.ds(0, ROWS)], dst.at[band, pl.ds(0, ROWS)], phase, to).start()
            return carry

        lax.fori_loop(0, BANDS - 1, go, 0)
        dst[band] = src[band]

    def wait_bytes(ref, sem):
        pltpu.make_async_copy(ref, ref, sem).wait()

    def lat_recv(dst, phase):
        wait_bytes(dst.at[pl.ds(0, BANDS - 1), pl.ds(0, ROWS)], recv_sem.at[phase])

    def lat_sent(src, phase):
        wait_bytes(src.at[pl.ds(0, BANDS - 1), pl.ds(0, ROWS)], send_sem.at[phase])

    def clear(buffer):
        buffer[:, ROWS:PAD, :] = jnp.zeros((BANDS, PAD - ROWS, NX), BF)

    cell = cell_ref[...]
    line = ((cell.astype(F32) + 0.5) * (1.0 / NX)).astype(jnp.int32)
    level = ((line.astype(F32) + 0.5) * (1.0 / ROWS)).astype(jnp.int32)
    col_ref[...] = cell - line * NX
    line_ref[...] = (line - level * ROWS) * LEV + level

    def scatter(target, with_innovation):
        target[...] = jnp.zeros((LINES, NX), F32)

        def step(k, carry):
            here = pl.ds(pl.multiple_of(k * CHUNK, CHUNK), CHUNK)
            values = accept_ref[:, here].astype(F32) * prec_ref[:, here]
            if with_innovation:
                values = values * innov_ref[:, here]
            high = values.astype(BF).astype(F32)
            at_line = iota((LINES, CHUNK), 0) == line_ref[:, here]
            at_col = (iota((NX, CHUNK), 0) == col_ref[:, here]).astype(F32).astype(BF)
            total = target[...]
            for piece in (high, values - high):
                picked = jnp.where(at_line, piece, 0.0).astype(BF)
                total = total + lax.dot_general(
                    picked, at_col, (((1,), (1,)), ((), ())), preferred_element_type=F32
                )
            target[...] = total
            return carry

        lax.fori_loop(0, OBS // CHUNK, step, 0)

    def spread_out(values, target):
        target[...] = dot(perm[...], values.astype(BF)).astype(BF).reshape(LEV, PAD, NX)

    def correlate(source, target):
        flat[...] = source[...].reshape(WIDE, NX)
        acc[...] = jnp.zeros((WIDE, NX), F32)

        def scale(s, carry):
            across[...] = dot(lat_tab[s], flat[...]).astype(BF)
            acc[...] += sw_ref[s] * dot(across[...], lon_tab[s])
            return carry

        lax.fori_loop(0, SCALES, scale, 0)
        target[...] = acc[...].astype(BF).reshape(LEV, PAD, NX)

    def mix(tables, source):
        flat[...] = source[...].reshape(WIDE, NX)
        return dot(tables[0], flat[...]) + dot(tables[1], flat[...])

    def build_perm():
        row, col = iota((WIDE, LINES), 0), iota((WIDE, LINES), 1)
        inner = row % PAD
        match = jnp.logical_and(inner < ROWS, inner * LEV + row // PAD == col)
        perm[...] = match.astype(F32).astype(BF)

    def build_tables():
        def lat(s, carry):
            row, col = iota((WIDE, WIDE), 0), iota((WIDE, WIDE), 1)
            valid = jnp.logical_and(row % PAD < ROWS, col % PAD < ROWS)
            gap = (row // PAD - col // PAD) * ROWS + row % PAD - col % PAD
            scaled = gap.astype(F32) / latlen_ref[s]
            lat_tab[s] = jnp.where(valid, jnp.exp(-0.5 * scaled * scaled), 0.0).astype(BF)
            return carry

        lax.fori_loop(0, SCALES, lat, 0)

        def lon(s, carry):
            gap = jnp.abs(iota((NX, NX), 0) - iota((NX, NX), 1))
            scaled = jnp.minimum(gap, NX - gap).astype(F32) / lonlen_ref[s]
            lon_tab[s] = jnp.exp(-0.5 * scaled * scaled).astype(BF)
            return carry

        lax.fori_loop(0, SCALES, lon, 0)
        vert = vert_ref[...]
        both = lax.dot_general(
            vert,
            vert,
            (((1,), (1,)), ((), ())),
            precision=lax.Precision.HIGHEST,
            preferred_element_type=F32,
        )
        pick_row = (iota((LINES, LEV), 0) % LEV == iota((LINES, LEV), 1)).astype(F32).astype(BF)
        pick_col = (iota((LEV, WIDE), 1) // PAD == iota((LEV, WIDE), 0)).astype(F32).astype(BF)
        same = iota((LINES, WIDE), 0) // LEV == iota((LINES, WIDE), 1) % PAD
        for matrix, target in ((vert.T, grad_mix), (both, image_mix)):
            high = matrix.astype(BF)
            low = (matrix - high.astype(F32)).astype(BF)
            for index, piece in enumerate((high, low)):
                rows = dot(pick_row, piece).astype(BF)
                target[index] = jnp.where(same, -dot(rows, pick_col), 0.0).astype(BF)

    def pert():
        return pert_ref[...].astype(F32).reshape(LINES, NX)

    for buffer in (recv_x, recv_t, recv_u, recv_y, recv_r):
        clear(buffer)
    build_perm()
    scatter(field, True)
    spread_out(pert() * field[...], send_x)
    pl.semaphore_wait(barrier, BANDS - 1 + MEMS - 1)
    lat_start(send_x, recv_x, X1)
    build_tables()
    scatter(weight, False)
    lat_recv(recv_x, X1)
    correlate(recv_x, send_t)
    correlate(send_t, send_u)
    lat_start(send_u, recv_u, UU)
    lat_start(send_t, recv_t, TT)
    lat_recv(recv_u, UU)

    part[...] = (pert() * mix(image_mix, recv_u)).reshape(ROWS, MEMS, LEV // MEMS, NX).astype(BF)

    def share(k, carry):
        other, to = mem_peer(k)
        remote(part.at[:, other], part_in.at[mem], RS, to).start()
        return carry

    lax.fori_loop(1, MEMS, share, 0)
    part_in[mem] = part[:, mem]
    wait_bytes(part_in.at[pl.ds(0, MEMS - 1)], recv_sem.at[RS])
    own[...] = jnp.sum(part_in[...].astype(F32), axis=0).astype(BF)

    def gather(k, carry):
        _, to = mem_peer(k)
        remote(own, image.at[:, mem], AG, to).start()
        return carry

    lax.fori_loop(1, MEMS, gather, 0)
    image[:, mem] = own[...]
    wait_bytes(image.at[:, pl.ds(0, MEMS - 1)], recv_sem.at[AG])
    field[...] = image[...].astype(F32).reshape(LINES, NX)
    spread_out(pert() * (weight[...] * field[...]), send_y)
    lat_start(send_y, recv_y, X2)
    obs_square = jnp.sum(weight[...] * field[...] * field[...])
    obs_square = jnp.where(mem == 0, obs_square, 0.0)
    lat_recv(recv_t, TT)
    f_ref[...] = mix(grad_mix, recv_t)
    grad_square = jnp.sum(f_ref[...] * f_ref[...])
    lat_recv(recv_y, X2)
    correlate(recv_y, send_r)
    lat_start(send_r, recv_r, RR)
    lat_recv(recv_r, RR)
    h_ref[...] = -mix(grad_mix, recv_r)
    cross = jnp.sum(f_ref[...] * h_ref[...])
    hess_square = jnp.sum(h_ref[...] * h_ref[...])

    lane = iota((1, 128), 1)
    row = jnp.zeros((1, 128), F32)
    for index, value in enumerate((grad_square, cross, hess_square, obs_square)):
        row = jnp.where(lane == index, value, row)
    row_mem[...] = row

    def tell_mem(k, carry):
        _, to = mem_peer(k)
        remote(row_mem, sums_mem.at[mem], SM, to).start()
        return carry

    lax.fori_loop(1, MEMS, tell_mem, 0)
    sums_mem[mem] = row
    wait_bytes(sums_mem.at[pl.ds(0, MEMS - 1)], recv_sem.at[SM])
    row = jnp.sum(sums_mem[...], axis=0)
    row_lat[...] = row

    def tell_lat(k, carry):
        _, to = lat_peer(k)
        remote(row_lat, sums_lat.at[band], SL, to).start()
        return carry

    lax.fori_loop(0, BANDS - 1, tell_lat, 0)
    sums_lat[band] = row
    wait_bytes(sums_lat.at[pl.ds(0, BANDS - 1)], recv_sem.at[SL])
    sums_ref[...] = jnp.sum(sums_lat[...], axis=0)

    for buffer, phase in ((send_x, X1), (send_u, UU), (send_t, TT), (send_y, X2), (send_r, RR)):
        lat_sent(buffer, phase)
    wait_bytes(part_in.at[pl.ds(0, MEMS - 1)], send_sem.at[RS])
    wait_bytes(image.at[:, pl.ds(0, MEMS - 1)], send_sem.at[AG])
    wait_bytes(sums_mem.at[pl.ds(0, MEMS - 1)], send_sem.at[SM])
    wait_bytes(sums_lat.at[pl.ds(0, BANDS - 1)], send_sem.at[SL])


def local(
    ens_perts,
    vert_loc,
    lat_lengths,
    lon_lengths,
    scale_weights,
    obs_cell,
    obs_accept,
    innovation,
    obs_precision,
):
    vmem = pl.BlockSpec(memory_space=pltpu.VMEM)
    smem = pl.BlockSpec(memory_space=pltpu.SMEM)
    slab = pltpu.VMEM((BANDS, PAD, NX), BF)
    lines = pltpu.VMEM((LINES, NX), F32)
    grad, hess, sums = pl.pallas_call(
        kernel,
        out_shape=(
            jax.ShapeDtypeStruct((LINES, NX), F32),
            jax.ShapeDtypeStruct((LINES, NX), F32),
            jax.ShapeDtypeStruct((1, 128), F32),
        ),
        in_specs=[vmem, vmem, smem, smem, smem, vmem, vmem, vmem, vmem],
        out_specs=(vmem, vmem, vmem),
        scratch_shapes=[
            pltpu.VMEM((WIDE, LINES), BF),
            pltpu.VMEM((SCALES, WIDE, WIDE), BF),
            pltpu.VMEM((SCALES, NX, NX), BF),
            pltpu.VMEM((2, LINES, WIDE), BF),
            pltpu.VMEM((2, LINES, WIDE), BF),
            pltpu.VMEM((1, OBS), jnp.int32),
            pltpu.VMEM((1, OBS), jnp.int32),
            lines,
            lines,
            pltpu.VMEM((WIDE, NX), F32),
            pltpu.VMEM((WIDE, NX), BF),
            pltpu.VMEM((WIDE, NX), BF),
            slab,
            slab,
            slab,
            slab,
            slab,
            slab,
            slab,
            slab,
            slab,
            slab,
            pltpu.VMEM((ROWS, MEMS, LEV // MEMS, NX), BF),
            pltpu.VMEM((MEMS, ROWS, LEV // MEMS, NX), BF),
            pltpu.VMEM((ROWS, LEV // MEMS, NX), BF),
            pltpu.VMEM((ROWS, MEMS, LEV // MEMS, NX), BF),
            pltpu.VMEM((1, 128), F32),
            pltpu.VMEM((1, 128), F32),
            pltpu.VMEM((MEMS, 1, 128), F32),
            pltpu.VMEM((BANDS, 1, 128), F32),
            pltpu.SemaphoreType.DMA((9,)),
            pltpu.SemaphoreType.DMA((9,)),
        ],
        compiler_params=pltpu.CompilerParams(
            collective_id=0, has_side_effects=True, vmem_limit_bytes=60 * 1024 * 1024
        ),
    )(
        ens_perts[0].transpose(1, 0, 2),
        vert_loc,
        lat_lengths,
        lon_lengths,
        scale_weights,
        obs_cell.reshape(1, OBS),
        obs_accept.reshape(1, OBS),
        innovation.reshape(1, OBS),
        obs_precision.reshape(1, OBS),
    )
    grad_square, cross, hess_square, obs_square = sums[0, 0], sums[0, 1], sums[0, 2], sums[0, 3]
    first_step = grad_square / (grad_square + obs_square)
    second_step = (grad_square + cross) / (grad_square + 2.0 * cross + hess_square)
    gradient = grad - first_step * (grad + hess)
    new_control = -first_step * grad - second_step * gradient

    def placed(field):
        return field.reshape(ROWS, LEV, NX).transpose(1, 0, 2)[None]

    return (placed(new_control), placed(gradient))


def solution(mesh):
    split = Mesh(mesh.devices.reshape(NZ, NYC, NXC, NC), ("lat_0", "lat_1", "mem_0", "mem_1"))
    placed = (P(MEM, None, LAT, None), P(), P(), P(), P(), P(LAT), P(LAT), P(LAT), P(LAT))
    return jax.shard_map(
        local,
        mesh=split,
        in_specs=placed,
        out_specs=(P(MEM, None, LAT, None), P(MEM, None, LAT, None)),
        check_vma=False,
    )
```

time: 661 us -> 201 us (0.30)
  blocking collectives: 291 us -> 0 us
  Pallas kernels: 0 us -> 191 us
  local copies, waits for them, and re-layouts: 131 us -> 1.41 us
  other arithmetic: 112 us -> 3.28 us
  matrix products: 42.3 us -> 0 us
  waiting for transfers between devices: 40.9 us -> 0 us
  starting transfers between devices: 35.4 us -> 0 us
    pallas_call x0 -> x1, Pallas kernels: none -> 191 us  [local(): pl.pallas_call(kernel, out_shape=(jax.ShapeDtypeStruct((LINES, NX), F32),...]
    all_to_all x4 -> x0, blocking collectives: 180 us -> none  [the longest x2 99.5 us: band_correlate(): lax.all_to_all(band_field, LAT, split_axis=1, concat_axis=2, tiled=True)]
    psum x8 -> x0, blocking collectives: 111 us -> none  [one_axis_at_a_time(): return functools.reduce(lax.psum, axes, array)]
    gather x2 -> x0, local copies, waits for them, and re-layouts: 101 us -> none  [the longest x1 50.7 us: local(): corr.reshape(members, cell_count)[:, obs_cell].astype(jnp.float32)]
    scatter-add x2 -> x0, other arithmetic: 87.7 us -> none  [adjoint(): spread = jnp.zeros((cell_count,), jnp.float32).at[obs_cell].add(obs_value...]
    dot_general x12 -> x0, matrix products: 42.3 us -> none  [the longest x9 38 us: correlate(): jnp.einsum('mlac,cd->mlad', across, lon_corr[scale_index], preferred_elem...]
    all_to_all x3 -> x0, waiting for transfers between devices: 40.9 us -> none  [the longest x1 35.6 us: band_correlate(): lax.all_to_all(band_field, LAT, split_axis=1, concat_axis=2, tiled=True)]
    all_to_all x3 -> x0, starting transfers between devices: 35.4 us -> none  [the longest x1 19.6 us: band_correlate(): lax.all_to_all(band_field, LAT, split_axis=1, concat_axis=2, tiled=True)]
  transfers between devices with their start and end apart: 3 -> 0, of which waited for: 2 -> 0; matrix products, arithmetic and copies ran while one was open for 9% -> 0% of each run, Pallas kernels for 0% -> 0%
where the time goes in v1:
time: 201 us
  Pallas kernels  191 us (95%)
  between operations  5.59 us (3%)
  other arithmetic  3.28 us (2%)
    pallas_call x1, Pallas kernels, local(): pl.pallas_call(kernel, out_shape=(jax.ShapeDtypeStruct((LINES, NX), F32),...  191 us

profile of v1, /device:TPU:1, one launch (start us, length us, event | category | flops | bytes accessed | tf_op | source)
XLA Modules:
  0.0 201.1 jit_solution(10870087234239641220)
XLA Ops:
  0.6 190.9 %shard_map.104 = (f32[384,768]{1,0:T(8,128)}, f32[384,768]{1,0:T(8,128)}, f32[1,128]{1,0:T(1,128)}) custom-call(bf16[6,64,768]{2,1,0:T(8,128)(2,1)} %bitcast.23, f32[64,64]{1,0:T(8,128)} %vert_ref.1, f32[3]{0:T(128)} %latlen_ref.1, f32[3]{0:T(128)} %lonlen_ref.1, f32[3]{0:T(128)} %sw_ref.1, s32[1,8192]{1,0:T(1,128)} %bitcast.24, s32[1,8192]{1,0:T(1,128)} %bitcast.25, ...), custom_call_target="tpu_custom_call" | custom-call | tf_op jit(solution)/shard_map/pallas_call | solution.py:340
  191.5 1.4 fusion
  197.9 3.3 %multiply_subtract_fusion = (f32[384,768]{1,0:T(8,128)}, f32[384,768]{1,0:T(8,128)}) fusion(f32[384,768]{1,0:T(8,128)} %get-tuple-element.6, f32[]{:T(128)S(6)} %div.7, f32[]{:T(128)S(6)} %neg.3, f32[384,768]{1,0:T(8,128)} %get-tuple-element.7, f32[]{:T(128)S(6)} %div.6), kind=kLoop, calls=%fused_computation | loop fusion | flops 1769472 | bytes 4718604 | tf_op jit(solution)/shard_map/sub | solution.py:401

commit v2 on v1

--- a/solution.py
+++ b/solution.py
@@ -20,6 +20,8 @@
 WIDE = LEV * PAD
 SCALES = 3
 OBS = 8192
+BLOCK = 256
+EDGE = 128
 CHUNK = 512
 BF = jnp.bfloat16
 F32 = jnp.float32
@@ -45,9 +47,8 @@
     accept_ref,
     innov_ref,
     prec_ref,
-    f_ref,
-    h_ref,
-    sums_ref,
+    control_ref,
+    gradient_ref,
     perm,
     lat_tab,
     lon_tab,
@@ -74,6 +75,8 @@
     part_in,
     own,
     image,
+    f_ref,
+    h_ref,
     row_mem,
     row_lat,
     sums_mem,
@@ -161,7 +164,7 @@
             at_line = iota((LINES, CHUNK), 0) == line_ref[:, here]
             at_col = (iota((NX, CHUNK), 0) == col_ref[:, here]).astype(F32).astype(BF)
             total = target[...]
-            for piece in (high, values - high):
+            for piece in (high,) if with_innovation else (high, values - high):
                 picked = jnp.where(at_line, piece, 0.0).astype(BF)
                 total = total + lax.dot_general(
                     picked, at_col, (((1,), (1,)), ((), ())), preferred_element_type=F32
@@ -179,8 +182,13 @@
         acc[...] = jnp.zeros((WIDE, NX), F32)
 
         def scale(s, carry):
-            across[...] = dot(lat_tab[s], flat[...]).astype(BF)
-            acc[...] += sw_ref[s] * dot(across[...], lon_tab[s])
+            rows = dot(lat_tab[s], flat[...]).astype(BF)
+            across[:, EDGE : EDGE + NX] = rows
+            across[:, :EDGE] = rows[:, NX - EDGE :]
+            across[:, EDGE + NX :] = rows[:, :EDGE]
+            for first in range(0, NX, BLOCK):
+                window = across[:, first : first + BLOCK + 2 * EDGE]
+                acc[:, first : first + BLOCK] += sw_ref[s] * dot(window, lon_tab[s])
             return carry
 
         lax.fori_loop(0, SCALES, scale, 0)
@@ -208,8 +216,9 @@
         lax.fori_loop(0, SCALES, lat, 0)
 
         def lon(s, carry):
-            gap = jnp.abs(iota((NX, NX), 0) - iota((NX, NX), 1))
-            scaled = jnp.minimum(gap, NX - gap).astype(F32) / lonlen_ref[s]
+            tall = (BLOCK + 2 * EDGE, BLOCK)
+            gap = iota(tall, 0) - EDGE - iota(tall, 1)
+            scaled = gap.astype(F32) / lonlen_ref[s]
             lon_tab[s] = jnp.exp(-0.5 * scaled * scaled).astype(BF)
             return carry
 
@@ -243,12 +252,12 @@
     pl.semaphore_wait(barrier, BANDS - 1 + MEMS - 1)
     lat_start(send_x, recv_x, X1)
     build_tables()
-    scatter(weight, False)
     lat_recv(recv_x, X1)
     correlate(recv_x, send_t)
     correlate(send_t, send_u)
     lat_start(send_u, recv_u, UU)
     lat_start(send_t, recv_t, TT)
+    scatter(weight, False)
     lat_recv(recv_u, UU)
 
     part[...] = (pert() * mix(image_mix, recv_u)).reshape(ROWS, MEMS, LEV // MEMS, NX).astype(BF)
@@ -312,7 +321,15 @@
     lax.fori_loop(0, BANDS - 1, tell_lat, 0)
     sums_lat[band] = row
     wait_bytes(sums_lat.at[pl.ds(0, BANDS - 1)], recv_sem.at[SL])
-    sums_ref[...] = jnp.sum(sums_lat[...], axis=0)
+    total = jnp.sum(sums_lat[...], axis=0)
+    grad_square, cross, hess_square, obs_square = (
+        jnp.sum(jnp.where(lane == index, total, 0.0)) for index in range(4)
+    )
+    first_step = grad_square / (grad_square + obs_square)
+    second_step = (grad_square + cross) / (grad_square + 2.0 * cross + hess_square)
+    gradient = f_ref[...] - first_step * (f_ref[...] + h_ref[...])
+    gradient_ref[...] = gradient
+    control_ref[...] = -first_step * f_ref[...] - second_step * gradient
 
     for buffer, phase in ((send_x, X1), (send_u, UU), (send_t, TT), (send_y, X2), (send_r, RR)):
         lat_sent(buffer, phase)
@@ -337,19 +354,18 @@
     smem = pl.BlockSpec(memory_space=pltpu.SMEM)
     slab = pltpu.VMEM((BANDS, PAD, NX), BF)
     lines = pltpu.VMEM((LINES, NX), F32)
-    grad, hess, sums = pl.pallas_call(
+    new_control, gradient = pl.pallas_call(
         kernel,
         out_shape=(
             jax.ShapeDtypeStruct((LINES, NX), F32),
             jax.ShapeDtypeStruct((LINES, NX), F32),
-            jax.ShapeDtypeStruct((1, 128), F32),
         ),
         in_specs=[vmem, vmem, smem, smem, smem, vmem, vmem, vmem, vmem],
-        out_specs=(vmem, vmem, vmem),
+        out_specs=(vmem, vmem),
         scratch_shapes=[
             pltpu.VMEM((WIDE, LINES), BF),
             pltpu.VMEM((SCALES, WIDE, WIDE), BF),
-            pltpu.VMEM((SCALES, NX, NX), BF),
+            pltpu.VMEM((SCALES, BLOCK + 2 * EDGE, BLOCK), BF),
             pltpu.VMEM((2, LINES, WIDE), BF),
             pltpu.VMEM((2, LINES, WIDE), BF),
             pltpu.VMEM((1, OBS), jnp.int32),
@@ -357,7 +373,7 @@
             lines,
             lines,
             pltpu.VMEM((WIDE, NX), F32),
-            pltpu.VMEM((WIDE, NX), BF),
+            pltpu.VMEM((WIDE, NX + 2 * EDGE), BF),
             pltpu.VMEM((WIDE, NX), BF),
             slab,
             slab,
@@ -373,6 +389,8 @@
             pltpu.VMEM((MEMS, ROWS, LEV // MEMS, NX), BF),
             pltpu.VMEM((ROWS, LEV // MEMS, NX), BF),
             pltpu.VMEM((ROWS, MEMS, LEV // MEMS, NX), BF),
+            lines,
+            lines,
             pltpu.VMEM((1, 128), F32),
             pltpu.VMEM((1, 128), F32),
             pltpu.VMEM((MEMS, 1, 128), F32),
@@ -381,7 +399,7 @@
             pltpu.SemaphoreType.DMA((9,)),
         ],
         compiler_params=pltpu.CompilerParams(
-            collective_id=0, has_side_effects=True, vmem_limit_bytes=60 * 1024 * 1024
+            collective_id=0, has_side_effects=True, vmem_limit_bytes=40 * 1024 * 1024
         ),
     )(
         ens_perts[0].transpose(1, 0, 2),
@@ -394,11 +412,6 @@
         innovation.reshape(1, OBS),
         obs_precision.reshape(1, OBS),
     )
-    grad_square, cross, hess_square, obs_square = sums[0, 0], sums[0, 1], sums[0, 2], sums[0, 3]
-    first_step = grad_square / (grad_square + obs_square)
-    second_step = (grad_square + cross) / (grad_square + 2.0 * cross + hess_square)
-    gradient = grad - first_step * (grad + hess)
-    new_control = -first_step * grad - second_step * gradient
 
     def placed(field):
         return field.reshape(ROWS, LEV, NX).transpose(1, 0, 2)[None]

time: 201 us -> 194 us (0.965)
  local copies, waits for them, and re-layouts: 1.41 us -> 8.84 us
  Pallas kernels: 191 us -> 184 us
  between operations: 5.59 us -> 0.66 us
  other arithmetic: 3.28 us -> 0 us
    unnamed x0 -> x20, local copies, waits for them, and re-layouts: none -> 8.84 us
    pallas_call x1, Pallas kernels: 191 us -> 184 us  [local(): pl.pallas_call(kernel, out_shape=(jax.ShapeDtypeStruct((LINES, NX), F32),...]
    sub x1 -> x0, other arithmetic: 3.28 us -> none  [local(): new_control = -first_step * grad - second_step * gradient]
where the time goes in v2:
time: 194 us; the launch traced here: 193 us
  Pallas kernels  184 us (95%)
  local copies, waits for them, and re-layouts  8.84 us (5%)
    pallas_call x1, Pallas kernels, local(): pl.pallas_call(kernel, out_shape=(jax.ShapeDtypeStruct((LINES, NX), F32),...  184 us
    unnamed x20, local copies, waits for them, and re-layouts  8.84 us

profile of v2, /device:TPU:1, one launch (start us, length us, event | category | flops | bytes accessed | tf_op | source)
XLA Modules:
  0.0 193.4 jit_solution(3052043888019986758)
XLA Ops:
  0.6 0.0 copy-start
  0.6 1.1 copy-done
  1.7 0.0 copy-start.1
  1.7 0.8 copy-done.1
  2.5 0.0 copy-start.2
  2.5 0.8 copy-done.2
  3.2 0.0 copy-start.3
  3.2 0.8 copy-done.3
  4.0 0.0 copy-start.4
  4.0 0.8 copy-done.4
  4.7 0.0 copy-start.5
  4.7 0.8 copy-done.5
  5.5 0.0 copy-start.6
  5.5 0.7 copy-done.6
  6.1 0.0 copy-start.7
  6.1 0.7 copy-done.7
  6.8 0.0 copy-start.8
  6.8 0.7 copy-done.8
  7.5 183.9 %shard_map.104 = (f32[384,768]{1,0:T(8,128)S(1)}, f32[384,768]{1,0:T(8,128)S(1)}) custom-call(bf16[6,64,768]{2,1,0:T(8,128)(2,1)S(1)} %bitcast.19, f32[64,64]{1,0:T(8,128)S(1)} %copy-done.1, f32[3]{0:T(128)S(1)} %copy-done.6, f32[3]{0:T(128)S(1)} %copy-done.7, f32[3]{0:T(128)S(1)} %copy-done.8, s32[1,8192]{1,0:T(1,128)S(1)} %bitcast.20, ...), custom_call_target="tpu_custom_call" | custom-call | tf_op jit(solution)/shard_map/pallas_call | solution.py:357
  191.3 1.0 copy.13
  192.4 1.0 copy.14
Async XLA Ops:
  0.6 1.1 copy-start
  1.7 0.8 copy-start.1
  2.5 0.8 copy-start.2
  3.2 0.8 copy-start.3
  4.0 0.8 copy-start.4
  4.7 0.8 copy-start.5
  5.5 0.7 copy-start.6
  6.1 0.7 copy-start.7
  6.8 0.7 copy-start.8

commit v3 on v2

--- a/solution.py
+++ b/solution.py
@@ -22,11 +22,14 @@
 OBS = 8192
 BLOCK = 256
 EDGE = 128
+TILE = 128
+TILES = NX // TILE
+NEAR = 20
 CHUNK = 512
 BF = jnp.bfloat16
 F32 = jnp.float32
 
-X1, UU, TT, X2, RR, RS, AG, SM, SL = range(9)
+PP, S1, A1, UU, TT, RS, S2, A2, RR, SM, SL = range(11)
 
 
 def iota(shape, dim):
@@ -56,25 +59,27 @@
     image_mix,
     line_ref,
     col_ref,
-    field,
+    spread,
     weight,
     acc,
     across,
     flat,
-    send_x,
+    send_p,
     send_t,
     send_u,
-    send_y,
     send_r,
-    recv_x,
+    recv_p,
     recv_t,
     recv_u,
-    recv_y,
     recv_r,
+    tile_out,
+    tile_in,
+    tiles,
+    tile_out_two,
+    tile_in_two,
+    tiles_two,
     part,
     part_in,
-    own,
-    image,
     f_ref,
     h_ref,
     row_mem,
@@ -125,14 +130,13 @@
             device_id_type=MESH_ID,
         )
 
-    def lat_start(src, dst, phase):
+    def lat_start(src, dst, phase, first=0, last=BANDS - 1):
         def go(k, carry):
             there, to = lat_peer(k)
             remote(src.at[there, pl.ds(0, ROWS)], dst.at[band, pl.ds(0, ROWS)], phase, to).start()
             return carry
 
-        lax.fori_loop(0, BANDS - 1, go, 0)
-        dst[band] = src[band]
+        lax.fori_loop(first, last, go, 0)
 
     def wait_bytes(ref, sem):
         pltpu.make_async_copy(ref, ref, sem).wait()
@@ -144,16 +148,17 @@
         wait_bytes(src.at[pl.ds(0, BANDS - 1), pl.ds(0, ROWS)], send_sem.at[phase])
 
     def clear(buffer):
-        buffer[:, ROWS:PAD, :] = jnp.zeros((BANDS, PAD - ROWS, NX), BF)
+        shape = (BANDS, PAD - ROWS, buffer.shape[-1])
+        buffer[:, ROWS:PAD, :] = jnp.zeros(shape, BF)
 
     cell = cell_ref[...]
     line = ((cell.astype(F32) + 0.5) * (1.0 / NX)).astype(jnp.int32)
     level = ((line.astype(F32) + 0.5) * (1.0 / ROWS)).astype(jnp.int32)
-    col_ref[...] = cell - line * NX
+    col_ref[...] = cell - line * NX - mem * TILE
     line_ref[...] = (line - level * ROWS) * LEV + level
 
     def scatter(target, with_innovation):
-        target[...] = jnp.zeros((LINES, NX), F32)
+        target[...] = jnp.zeros((LINES, TILE), F32)
 
         def step(k, carry):
             here = pl.ds(pl.multiple_of(k * CHUNK, CHUNK), CHUNK)
@@ -162,9 +167,9 @@
                 values = values * innov_ref[:, here]
             high = values.astype(BF).astype(F32)
             at_line = iota((LINES, CHUNK), 0) == line_ref[:, here]
-            at_col = (iota((NX, CHUNK), 0) == col_ref[:, here]).astype(F32).astype(BF)
+            at_col = (iota((TILE, CHUNK), 0) == col_ref[:, here]).astype(F32).astype(BF)
             total = target[...]
-            for piece in (high,) if with_innovation else (high, values - high):
+            for piece in (high, values - high):
                 picked = jnp.where(at_line, piece, 0.0).astype(BF)
                 total = total + lax.dot_general(
                     picked, at_col, (((1,), (1,)), ((), ())), preferred_element_type=F32
@@ -174,11 +179,37 @@
 
         lax.fori_loop(0, OBS // CHUNK, step, 0)
 
-    def spread_out(values, target):
-        target[...] = dot(perm[...], values.astype(BF)).astype(BF).reshape(LEV, PAD, NX)
-
-    def correlate(source, target):
-        flat[...] = source[...].reshape(WIDE, NX)
+    def by_level(values):
+        return dot(perm[...], values).astype(BF).reshape(LEV, PAD, values.shape[-1])
+
+    def tile_gather(out, inward, every, phase_lat, phase_mem):
+        @pl.when(mem < TILES)
+        def _():
+            lat_recv(inward, phase_lat)
+            inward[band] = out[band]
+
+            def go(k, carry):
+                _, to = mem_peer(k)
+                remote(
+                    inward.at[:, pl.ds(0, ROWS)], every.at[mem, :, pl.ds(0, ROWS)], phase_mem, to
+                ).start()
+                return carry
+
+            lax.fori_loop(1, MEMS, go, 0)
+            every[mem] = inward[...]
+            wait_bytes(every.at[pl.ds(0, TILES - 1), :, pl.ds(0, ROWS)], recv_sem.at[phase_mem])
+
+        @pl.when(mem >= TILES)
+        def _():
+            wait_bytes(every.at[pl.ds(0, TILES), :, pl.ds(0, ROWS)], recv_sem.at[phase_mem])
+
+    def owner_schur(every):
+        for t in range(TILES):
+            cols = slice(t * TILE, (t + 1) * TILE)
+            product = recv_p[:, :, cols].astype(F32) * every[t].astype(F32)
+            flat[:, cols] = product.astype(BF).reshape(WIDE, TILE)
+
+    def correlate(target):
         acc[...] = jnp.zeros((WIDE, NX), F32)
 
         def scale(s, carry):
@@ -244,53 +275,79 @@
     def pert():
         return pert_ref[...].astype(F32).reshape(LINES, NX)
 
-    for buffer in (recv_x, recv_t, recv_u, recv_y, recv_r):
+    for buffer in (recv_p, recv_t, recv_u, recv_r):
         clear(buffer)
+    for buffer in (tile_in, tile_in_two):
+        clear(buffer)
+    for every in (tiles, tiles_two):
+        for t in range(TILES):
+            clear(every.at[t])
     build_perm()
-    scatter(field, True)
-    spread_out(pert() * field[...], send_x)
+    scatter(spread, True)
+    tile_out[...] = by_level(spread[...].astype(BF))
     pl.semaphore_wait(barrier, BANDS - 1 + MEMS - 1)
-    lat_start(send_x, recv_x, X1)
+
+    @pl.when(mem < TILES)
+    def _():
+        lat_start(tile_out, tile_in, S1)
+
+    send_p[...] = by_level(pert_ref[...].reshape(LINES, NX))
+    lat_start(send_p, recv_p, PP)
     build_tables()
-    lat_recv(recv_x, X1)
-    correlate(recv_x, send_t)
-    correlate(send_t, send_u)
+    tile_gather(tile_out, tile_in, tiles, S1, A1)
+    scatter(weight, False)
+    recv_p[band] = send_p[band]
+    lat_recv(recv_p, PP)
+    owner_schur(tiles)
+    correlate(send_t)
+    flat[...] = send_t[...].reshape(WIDE, NX)
+    correlate(send_u)
     lat_start(send_u, recv_u, UU)
-    lat_start(send_t, recv_t, TT)
-    scatter(weight, False)
+    lat_start(send_t, recv_t, TT, 0, NEAR)
+    recv_u[band] = send_u[band]
+    recv_t[band] = send_t[band]
     lat_recv(recv_u, UU)
 
-    part[...] = (pert() * mix(image_mix, recv_u)).reshape(ROWS, MEMS, LEV // MEMS, NX).astype(BF)
+    partial = (pert() * mix(image_mix, recv_u)).astype(BF)
+    for t in range(TILES):
+        part[t] = partial[:, t * TILE : (t + 1) * TILE]
 
     def share(k, carry):
-        other, to = mem_peer(k)
-        remote(part.at[:, other], part_in.at[mem], RS, to).start()
+        there = (mem + k) % TILES
+
+        @pl.when(there != mem)
+        def _():
+            to = {"mem_0": there // NC, "mem_1": there % NC}
+            remote(part.at[there], part_in.at[mem], RS, to).start()
+
         return carry
 
-    lax.fori_loop(1, MEMS, share, 0)
-    part_in[mem] = part[:, mem]
-    wait_bytes(part_in.at[pl.ds(0, MEMS - 1)], recv_sem.at[RS])
-    own[...] = jnp.sum(part_in[...].astype(F32), axis=0).astype(BF)
-
-    def gather(k, carry):
-        _, to = mem_peer(k)
-        remote(own, image.at[:, mem], AG, to).start()
-        return carry
-
-    lax.fori_loop(1, MEMS, gather, 0)
-    image[:, mem] = own[...]
-    wait_bytes(image.at[:, pl.ds(0, MEMS - 1)], recv_sem.at[AG])
-    field[...] = image[...].astype(F32).reshape(LINES, NX)
-    spread_out(pert() * (weight[...] * field[...]), send_y)
-    lat_start(send_y, recv_y, X2)
-    obs_square = jnp.sum(weight[...] * field[...] * field[...])
-    obs_square = jnp.where(mem == 0, obs_square, 0.0)
+    lax.fori_loop(0, TILES, share, 0)
+
+    @pl.when(mem < TILES)
+    def _():
+        part_in[mem] = part[mem]
+        wait_bytes(part_in.at[pl.ds(0, MEMS - 1)], recv_sem.at[RS])
+        image = jnp.sum(part_in[...].astype(F32), axis=0)
+        weighted = weight[...] * image
+        spread[...] = weighted * image
+        tile_out_two[...] = by_level(weighted.astype(BF))
+        lat_start(tile_out_two, tile_in_two, S2)
+
+    @pl.when(mem >= TILES)
+    def _():
+        spread[...] = jnp.zeros((LINES, TILE), F32)
+
+    lat_start(send_t, recv_t, TT, NEAR, BANDS - 1)
+    obs_square = jnp.sum(spread[...])
+    tile_gather(tile_out_two, tile_in_two, tiles_two, S2, A2)
+    owner_schur(tiles_two)
+    correlate(send_r)
+    lat_start(send_r, recv_r, RR)
+    recv_r[band] = send_r[band]
     lat_recv(recv_t, TT)
     f_ref[...] = mix(grad_mix, recv_t)
     grad_square = jnp.sum(f_ref[...] * f_ref[...])
-    lat_recv(recv_y, X2)
-    correlate(recv_y, send_r)
-    lat_start(send_r, recv_r, RR)
     lat_recv(recv_r, RR)
     h_ref[...] = -mix(grad_mix, recv_r)
     cross = jnp.sum(f_ref[...] * h_ref[...])
@@ -331,10 +388,21 @@
     gradient_ref[...] = gradient
     control_ref[...] = -first_step * f_ref[...] - second_step * gradient
 
-    for buffer, phase in ((send_x, X1), (send_u, UU), (send_t, TT), (send_y, X2), (send_r, RR)):
+    for buffer, phase in ((send_p, PP), (send_u, UU), (send_t, TT), (send_r, RR)):
         lat_sent(buffer, phase)
-    wait_bytes(part_in.at[pl.ds(0, MEMS - 1)], send_sem.at[RS])
-    wait_bytes(image.at[:, pl.ds(0, MEMS - 1)], send_sem.at[AG])
+
+    @pl.when(mem < TILES)
+    def _():
+        lat_sent(tile_out, S1)
+        lat_sent(tile_out_two, S2)
+        for every, phase in ((tiles, A1), (tiles_two, A2)):
+            wait_bytes(every.at[pl.ds(0, MEMS - 1), :, pl.ds(0, ROWS)], send_sem.at[phase])
+        wait_bytes(part_in.at[pl.ds(0, TILES - 1)], send_sem.at[RS])
+
+    @pl.when(mem >= TILES)
+    def _():
+        wait_bytes(part_in.at[pl.ds(0, TILES)], send_sem.at[RS])
+
     wait_bytes(sums_mem.at[pl.ds(0, MEMS - 1)], send_sem.at[SM])
     wait_bytes(sums_lat.at[pl.ds(0, BANDS - 1)], send_sem.at[SL])
 
@@ -354,6 +422,9 @@
     smem = pl.BlockSpec(memory_space=pltpu.SMEM)
     slab = pltpu.VMEM((BANDS, PAD, NX), BF)
     lines = pltpu.VMEM((LINES, NX), F32)
+    chunk = pltpu.VMEM((LINES, TILE), F32)
+    level_tile = pltpu.VMEM((BANDS, PAD, TILE), BF)
+    all_tiles = pltpu.VMEM((MEMS, BANDS, PAD, TILE), BF)
     new_control, gradient = pl.pallas_call(
         kernel,
         out_shape=(
@@ -370,8 +441,8 @@
             pltpu.VMEM((2, LINES, WIDE), BF),
             pltpu.VMEM((1, OBS), jnp.int32),
             pltpu.VMEM((1, OBS), jnp.int32),
-            lines,
-            lines,
+            chunk,
+            chunk,
             pltpu.VMEM((WIDE, NX), F32),
             pltpu.VMEM((WIDE, NX + 2 * EDGE), BF),
             pltpu.VMEM((WIDE, NX), BF),
@@ -383,23 +454,25 @@
             slab,
             slab,
             slab,
-            slab,
-            slab,
-            pltpu.VMEM((ROWS, MEMS, LEV // MEMS, NX), BF),
-            pltpu.VMEM((MEMS, ROWS, LEV // MEMS, NX), BF),
-            pltpu.VMEM((ROWS, LEV // MEMS, NX), BF),
-            pltpu.VMEM((ROWS, MEMS, LEV // MEMS, NX), BF),
+            level_tile,
+            level_tile,
+            all_tiles,
+            level_tile,
+            level_tile,
+            all_tiles,
+            pltpu.VMEM((TILES, LINES, TILE), BF),
+            pltpu.VMEM((MEMS, LINES, TILE), BF),
             lines,
             lines,
             pltpu.VMEM((1, 128), F32),
             pltpu.VMEM((1, 128), F32),
             pltpu.VMEM((MEMS, 1, 128), F32),
             pltpu.VMEM((BANDS, 1, 128), F32),
-            pltpu.SemaphoreType.DMA((9,)),
-            pltpu.SemaphoreType.DMA((9,)),
+            pltpu.SemaphoreType.DMA((11,)),
+            pltpu.SemaphoreType.DMA((11,)),
         ],
         compiler_params=pltpu.CompilerParams(
-            collective_id=0, has_side_effects=True, vmem_limit_bytes=40 * 1024 * 1024
+            collective_id=0, has_side_effects=True, vmem_limit_bytes=62 * 1024 * 1024
         ),
     )(
         ens_perts[0].transpose(1, 0, 2),

time: 194 us -> 179 us (0.923)
  Pallas kernels: 184 us -> 174 us
  local copies, waits for them, and re-layouts: 8.84 us -> 3.5 us
    pallas_call x1, Pallas kernels: 184 us -> 174 us  [local(): pl.pallas_call(kernel, out_shape=(jax.ShapeDtypeStruct((LINES, NX), F32),...]
    unnamed x20 -> x4, local copies, waits for them, and re-layouts: 8.84 us -> 3.5 us
where the time goes in v3:
time: 179 us; the launch traced here: 178 us
  Pallas kernels  174 us (97%)
  local copies, waits for them, and re-layouts  3.5 us (2%)
    pallas_call x1, Pallas kernels, local(): pl.pallas_call(kernel, out_shape=(jax.ShapeDtypeStruct((LINES, NX), F32),...  174 us

profile of v3, /device:TPU:1, one launch (start us, length us, event | category | flops | bytes accessed | tf_op | source)
XLA Modules:
  0.0 177.8 jit_solution(11247704417221113987)
XLA Ops:
  0.6 173.6 %shard_map.104 = (f32[384,768]{1,0:T(8,128)}, f32[384,768]{1,0:T(8,128)}) custom-call(bf16[6,64,768]{2,1,0:T(8,128)(2,1)} %bitcast.19, f32[64,64]{1,0:T(8,128)} %vert_ref.1, f32[3]{0:T(128)} %latlen_ref.1, f32[3]{0:T(128)} %lonlen_ref.1, f32[3]{0:T(128)} %sw_ref.1, s32[1,8192]{1,0:T(1,128)} %bitcast.20, s32[1,8192]{1,0:T(1,128)} %bitcast.21, ...), custom_call_target="tpu_custom_call" | custom-call | tf_op jit(solution)/shard_map/pallas_call | solution.py:428
  174.3 0.0 copy-start
  174.3 2.5 %copy.13 = f32[1,64,6,768]{3,1,2,0:T(8,128)} copy(f32[1,64,6,768]{3,1,2,0:T(8,128)} %bitcast.18) | data formatting | bytes 2359296
  176.8 0.0 copy-done
  176.8 1.0 copy.14
Async XLA Ops:
  174.3 2.5 %copy-start = (f32[384,768]{1,0:T(8,128)S(1)}, f32[384,768]{1,0:T(8,128)}, u32[]{:S(2)}) copy-start(f32[384,768]{1,0:T(8,128)} %get-tuple-element.5) | copy-start | bytes 3538948

commit v4 on v3

--- a/solution.py
+++ b/solution.py
@@ -24,12 +24,15 @@
 EDGE = 128
 TILE = 128
 TILES = NX // TILE
-NEAR = 20
+GROUP = 256
+GROUPS = NX // GROUP
+EARLY = 4
+NEAR = 8
 CHUNK = 512
 BF = jnp.bfloat16
 F32 = jnp.float32
 
-PP, S1, A1, UU, TT, RS, S2, A2, RR, SM, SL = range(11)
+PP, S1, A1, TT, RS, S2, A2, RR, SM, SL, UU = range(11)
 
 
 def iota(shape, dim):
@@ -138,6 +141,18 @@
 
         lax.fori_loop(first, last, go, 0)
 
+    def group_start(src, dst, g):
+        cols = pl.ds(g * GROUP, GROUP)
+
+        def go(k, carry):
+            there, to = lat_peer(k)
+            remote(
+                src.at[there, pl.ds(0, ROWS), cols], dst.at[band, pl.ds(0, ROWS), cols], UU + g, to
+            ).start()
+            return carry
+
+        lax.fori_loop(0, BANDS - 1, go, 0)
+
     def wait_bytes(ref, sem):
         pltpu.make_async_copy(ref, ref, sem).wait()
 
@@ -300,32 +315,15 @@
     lat_recv(recv_p, PP)
     owner_schur(tiles)
     correlate(send_t)
+    lat_start(send_t, recv_t, TT, 0, EARLY)
     flat[...] = send_t[...].reshape(WIDE, NX)
     correlate(send_u)
-    lat_start(send_u, recv_u, UU)
-    lat_start(send_t, recv_t, TT, 0, NEAR)
+    for g in range(GROUPS):
+        group_start(send_u, recv_u, g)
     recv_u[band] = send_u[band]
     recv_t[band] = send_t[band]
-    lat_recv(recv_u, UU)
-
-    partial = (pert() * mix(image_mix, recv_u)).astype(BF)
-    for t in range(TILES):
-        part[t] = partial[:, t * TILE : (t + 1) * TILE]
-
-    def share(k, carry):
-        there = (mem + k) % TILES
-
-        @pl.when(there != mem)
-        def _():
-            to = {"mem_0": there // NC, "mem_1": there % NC}
-            remote(part.at[there], part_in.at[mem], RS, to).start()
-
-        return carry
-
-    lax.fori_loop(0, TILES, share, 0)
-
-    @pl.when(mem < TILES)
-    def _():
+
+    def image_step():
         part_in[mem] = part[mem]
         wait_bytes(part_in.at[pl.ds(0, MEMS - 1)], recv_sem.at[RS])
         image = jnp.sum(part_in[...].astype(F32), axis=0)
@@ -334,11 +332,38 @@
         tile_out_two[...] = by_level(weighted.astype(BF))
         lat_start(tile_out_two, tile_in_two, S2)
 
+    for g in range(GROUPS):
+        cols = slice(g * GROUP, (g + 1) * GROUP)
+        wait_bytes(recv_u.at[pl.ds(0, BANDS - 1), pl.ds(0, ROWS), cols], recv_sem.at[UU + g])
+        got = recv_u[:, :, cols].reshape(WIDE, GROUP)
+        mixed = dot(image_mix[0], got) + dot(image_mix[1], got)
+        partial = (pert_ref[:, :, cols].astype(F32).reshape(LINES, GROUP) * mixed).astype(BF)
+        for half in range(NC):
+            t = g * NC + half
+            part[t] = partial[:, half * TILE : (half + 1) * TILE]
+
+            @pl.when(mem != t)
+            def _():
+                to = {"mem_0": g, "mem_1": half}
+                remote(part.at[t], part_in.at[mem], RS, to).start()
+
+        if g > 0:
+            pl.when(x == g - 1)(image_step)
+
+    @pl.when(x == GROUPS - 1)
+    def _():
+        lat_start(send_t, recv_t, TT, EARLY, NEAR)
+        image_step()
+        lat_start(send_t, recv_t, TT, NEAR, BANDS - 1)
+
+    @pl.when(x != GROUPS - 1)
+    def _():
+        lat_start(send_t, recv_t, TT, EARLY, BANDS - 1)
+
     @pl.when(mem >= TILES)
     def _():
         spread[...] = jnp.zeros((LINES, TILE), F32)
 
-    lat_start(send_t, recv_t, TT, NEAR, BANDS - 1)
     obs_square = jnp.sum(spread[...])
     tile_gather(tile_out_two, tile_in_two, tiles_two, S2, A2)
     owner_schur(tiles_two)
@@ -388,8 +413,11 @@
     gradient_ref[...] = gradient
     control_ref[...] = -first_step * f_ref[...] - second_step * gradient
 
-    for buffer, phase in ((send_p, PP), (send_u, UU), (send_t, TT), (send_r, RR)):
+    for buffer, phase in ((send_p, PP), (send_t, TT), (send_r, RR)):
         lat_sent(buffer, phase)
+    for g in range(GROUPS):
+        cols = slice(g * GROUP, (g + 1) * GROUP)
+        wait_bytes(send_u.at[pl.ds(0, BANDS - 1), pl.ds(0, ROWS), cols], send_sem.at[UU + g])
 
     @pl.when(mem < TILES)
     def _():
@@ -468,8 +496,8 @@
             pltpu.VMEM((1, 128), F32),
             pltpu.VMEM((MEMS, 1, 128), F32),
             pltpu.VMEM((BANDS, 1, 128), F32),
-            pltpu.SemaphoreType.DMA((11,)),
-            pltpu.SemaphoreType.DMA((11,)),
+            pltpu.SemaphoreType.DMA((10 + GROUPS,)),
+            pltpu.SemaphoreType.DMA((10 + GROUPS,)),
         ],
         compiler_params=pltpu.CompilerParams(
             collective_id=0, has_side_effects=True, vmem_limit_bytes=62 * 1024 * 1024

time: 179 us -> 175 us (0.978)
  Pallas kernels: 174 us -> 171 us
    pallas_call x1, Pallas kernels: 174 us -> 171 us  [local(): pl.pallas_call(kernel, out_shape=(jax.ShapeDtypeStruct((LINES, NX), F32),...]
where the time goes in v4:
time: 175 us
  Pallas kernels  171 us (98%)
  local copies, waits for them, and re-layouts  3.5 us (2%)
    pallas_call x1, Pallas kernels, local(): pl.pallas_call(kernel, out_shape=(jax.ShapeDtypeStruct((LINES, NX), F32),...  171 us

profile of v4, /device:TPU:1, one launch (start us, length us, event | category | flops | bytes accessed | tf_op | source)
XLA Modules:
  0.0 174.8 jit_solution(2376836880897179687)
XLA Ops:
  0.6 170.7 %shard_map.104 = (f32[384,768]{1,0:T(8,128)}, f32[384,768]{1,0:T(8,128)}) custom-call(bf16[6,64,768]{2,1,0:T(8,128)(2,1)} %bitcast.19, f32[64,64]{1,0:T(8,128)} %vert_ref.1, f32[3]{0:T(128)} %latlen_ref.1, f32[3]{0:T(128)} %lonlen_ref.1, f32[3]{0:T(128)} %sw_ref.1, s32[1,8192]{1,0:T(1,128)} %bitcast.20, s32[1,8192]{1,0:T(1,128)} %bitcast.21, ...), custom_call_target="tpu_custom_call" | custom-call | tf_op jit(solution)/shard_map/pallas_call | solution.py:456
  171.3 0.0 copy-start
  171.3 2.5 %copy.13 = f32[1,64,6,768]{3,1,2,0:T(8,128)} copy(f32[1,64,6,768]{3,1,2,0:T(8,128)} %bitcast.18) | data formatting | bytes 2359296
  173.8 0.0 copy-done
  173.8 1.0 copy.14
Async XLA Ops:
  171.3 2.5 %copy-start = (f32[384,768]{1,0:T(8,128)S(1)}, f32[384,768]{1,0:T(8,128)}, u32[]{:S(2)}) copy-start(f32[384,768]{1,0:T(8,128)} %get-tuple-element.5) | copy-start | bytes 3538948

commit v5 on v4

--- a/solution.py
+++ b/solution.py
@@ -28,11 +28,12 @@
 GROUPS = NX // GROUP
 EARLY = 4
 NEAR = 8
+TAIL = 40
 CHUNK = 512
 BF = jnp.bfloat16
 F32 = jnp.float32
 
-PP, S1, A1, TT, RS, S2, A2, RR, SM, SL, UU = range(11)
+PP, S1, A1, B1, TT, RS, S2, A2, B2, RR, SM, SL, UU = range(13)
 
 
 def iota(shape, dim):
@@ -85,6 +86,7 @@
     part_in,
     f_ref,
     h_ref,
+    stats,
     row_mem,
     row_lat,
     sums_mem,
@@ -197,26 +199,38 @@
     def by_level(values):
         return dot(perm[...], values).astype(BF).reshape(LEV, PAD, values.shape[-1])
 
-    def tile_gather(out, inward, every, phase_lat, phase_mem):
+    def tile_gather(out, inward, every, phase_lat, phase_chip, phase_pair):
+        partner = {"mem_1": 1 - c}
+
+        def of(tile):
+            return every.at[tile, :, pl.ds(0, ROWS)]
+
+        def chips(count):
+            return every.at[pl.ds(0, count), :, pl.ds(0, ROWS)]
+
         @pl.when(mem < TILES)
         def _():
             lat_recv(inward, phase_lat)
             inward[band] = out[band]
-
-            def go(k, carry):
-                _, to = mem_peer(k)
-                remote(
-                    inward.at[:, pl.ds(0, ROWS)], every.at[mem, :, pl.ds(0, ROWS)], phase_mem, to
-                ).start()
-                return carry
-
-            lax.fori_loop(1, MEMS, go, 0)
+            mine = inward.at[:, pl.ds(0, ROWS)]
+            for k in range(1, NXC):
+                remote(mine, of(mem), phase_chip, {"mem_0": (x + k) % NXC}).start()
+            remote(mine, of(mem), phase_pair, partner).start()
             every[mem] = inward[...]
-            wait_bytes(every.at[pl.ds(0, TILES - 1), :, pl.ds(0, ROWS)], recv_sem.at[phase_mem])
+            wait_bytes(chips(GROUPS - 1), recv_sem.at[phase_chip])
 
         @pl.when(mem >= TILES)
         def _():
-            wait_bytes(every.at[pl.ds(0, TILES), :, pl.ds(0, ROWS)], recv_sem.at[phase_mem])
+            wait_bytes(chips(GROUPS), recv_sem.at[phase_chip])
+
+        for g in range(GROUPS):
+
+            @pl.when(x != g)
+            def _():
+                there = g * NC + c
+                remote(of(there), of(there), phase_pair, partner).start()
+
+        wait_bytes(chips(GROUPS), recv_sem.at[phase_pair])
 
     def owner_schur(every):
         for t in range(TILES):
@@ -297,6 +311,8 @@
     for every in (tiles, tiles_two):
         for t in range(TILES):
             clear(every.at[t])
+    lane = iota((1, 128), 1)
+    stats[...] = jnp.zeros((1, 128), F32)
     build_perm()
     scatter(spread, True)
     tile_out[...] = by_level(spread[...].astype(BF))
@@ -309,7 +325,7 @@
     send_p[...] = by_level(pert_ref[...].reshape(LINES, NX))
     lat_start(send_p, recv_p, PP)
     build_tables()
-    tile_gather(tile_out, tile_in, tiles, S1, A1)
+    tile_gather(tile_out, tile_in, tiles, S1, A1, B1)
     scatter(weight, False)
     recv_p[band] = send_p[band]
     lat_recv(recv_p, PP)
@@ -328,7 +344,9 @@
         wait_bytes(part_in.at[pl.ds(0, MEMS - 1)], recv_sem.at[RS])
         image = jnp.sum(part_in[...].astype(F32), axis=0)
         weighted = weight[...] * image
-        spread[...] = weighted * image
+        square = jnp.sum(weighted * image)
+        first = -jnp.sum(spread[...] * image)
+        stats[...] = jnp.where(lane == 0, first, jnp.where(lane == 1, square, 0.0))
         tile_out_two[...] = by_level(weighted.astype(BF))
         lat_start(tile_out_two, tile_in_two, S2)
 
@@ -354,34 +372,21 @@
     def _():
         lat_start(send_t, recv_t, TT, EARLY, NEAR)
         image_step()
-        lat_start(send_t, recv_t, TT, NEAR, BANDS - 1)
+        lat_start(send_t, recv_t, TT, NEAR, TAIL)
 
     @pl.when(x != GROUPS - 1)
     def _():
-        lat_start(send_t, recv_t, TT, EARLY, BANDS - 1)
-
-    @pl.when(mem >= TILES)
-    def _():
-        spread[...] = jnp.zeros((LINES, TILE), F32)
-
-    obs_square = jnp.sum(spread[...])
-    tile_gather(tile_out_two, tile_in_two, tiles_two, S2, A2)
+        lat_start(send_t, recv_t, TT, EARLY, TAIL)
+
+    tile_gather(tile_out_two, tile_in_two, tiles_two, S2, A2, B2)
     owner_schur(tiles_two)
     correlate(send_r)
     lat_start(send_r, recv_r, RR)
+    lat_start(send_t, recv_t, TT, TAIL, BANDS - 1)
     recv_r[band] = send_r[band]
-    lat_recv(recv_t, TT)
-    f_ref[...] = mix(grad_mix, recv_t)
-    grad_square = jnp.sum(f_ref[...] * f_ref[...])
     lat_recv(recv_r, RR)
     h_ref[...] = -mix(grad_mix, recv_r)
-    cross = jnp.sum(f_ref[...] * h_ref[...])
-    hess_square = jnp.sum(h_ref[...] * h_ref[...])
-
-    lane = iota((1, 128), 1)
-    row = jnp.zeros((1, 128), F32)
-    for index, value in enumerate((grad_square, cross, hess_square, obs_square)):
-        row = jnp.where(lane == index, value, row)
+    row = jnp.where(lane == 2, jnp.sum(h_ref[...] * h_ref[...]), stats[...])
     row_mem[...] = row
 
     def tell_mem(k, carry):
@@ -402,13 +407,15 @@
 
     lax.fori_loop(0, BANDS - 1, tell_lat, 0)
     sums_lat[band] = row
+    lat_recv(recv_t, TT)
+    f_ref[...] = mix(grad_mix, recv_t)
     wait_bytes(sums_lat.at[pl.ds(0, BANDS - 1)], recv_sem.at[SL])
     total = jnp.sum(sums_lat[...], axis=0)
-    grad_square, cross, hess_square, obs_square = (
-        jnp.sum(jnp.where(lane == index, total, 0.0)) for index in range(4)
+    grad_square, obs_square, hess_square = (
+        jnp.sum(jnp.where(lane == index, total, 0.0)) for index in range(3)
     )
     first_step = grad_square / (grad_square + obs_square)
-    second_step = (grad_square + cross) / (grad_square + 2.0 * cross + hess_square)
+    second_step = (grad_square + obs_square) / (grad_square + 2.0 * obs_square + hess_square)
     gradient = f_ref[...] - first_step * (f_ref[...] + h_ref[...])
     gradient_ref[...] = gradient
     control_ref[...] = -first_step * f_ref[...] - second_step * gradient
@@ -424,8 +431,11 @@
         lat_sent(tile_out, S1)
         lat_sent(tile_out_two, S2)
         for every, phase in ((tiles, A1), (tiles_two, A2)):
-            wait_bytes(every.at[pl.ds(0, MEMS - 1), :, pl.ds(0, ROWS)], send_sem.at[phase])
+            wait_bytes(every.at[pl.ds(0, NXC - 1), :, pl.ds(0, ROWS)], send_sem.at[phase])
         wait_bytes(part_in.at[pl.ds(0, TILES - 1)], send_sem.at[RS])
+
+    for every, phase in ((tiles, B1), (tiles_two, B2)):
+        wait_bytes(every.at[pl.ds(0, GROUPS), :, pl.ds(0, ROWS)], send_sem.at[phase])
 
     @pl.when(mem >= TILES)
     def _():
@@ -494,10 +504,11 @@
             lines,
             pltpu.VMEM((1, 128), F32),
             pltpu.VMEM((1, 128), F32),
+            pltpu.VMEM((1, 128), F32),
             pltpu.VMEM((MEMS, 1, 128), F32),
             pltpu.VMEM((BANDS, 1, 128), F32),
-            pltpu.SemaphoreType.DMA((10 + GROUPS,)),
-            pltpu.SemaphoreType.DMA((10 + GROUPS,)),
+            pltpu.SemaphoreType.DMA((12 + GROUPS,)),
+            pltpu.SemaphoreType.DMA((12 + GROUPS,)),
         ],
         compiler_params=pltpu.CompilerParams(
             collective_id=0, has_side_effects=True, vmem_limit_bytes=62 * 1024 * 1024

time: 175 us -> 172 us (0.983)
  Pallas kernels: 171 us -> 168 us
    pallas_call x1, Pallas kernels: 171 us -> 168 us  [local(): pl.pallas_call(kernel, out_shape=(jax.ShapeDtypeStruct((LINES, NX), F32),...]
where the time goes in v5:
time: 172 us
  Pallas kernels  168 us (98%)
  local copies, waits for them, and re-layouts  3.5 us (2%)
    pallas_call x1, Pallas kernels, local(): pl.pallas_call(kernel, out_shape=(jax.ShapeDtypeStruct((LINES, NX), F32),...  168 us
    unnamed x4, local copies, waits for them, and re-layouts  3.5 us

profile of v5, /device:TPU:1, one launch (start us, length us, event | category | flops | bytes accessed | tf_op | source)
XLA Modules:
  0.0 172.2 jit_solution(17284908300563034003)
XLA Ops:
  0.6 168.0 %shard_map.104 = (f32[384,768]{1,0:T(8,128)}, f32[384,768]{1,0:T(8,128)}) custom-call(bf16[6,64,768]{2,1,0:T(8,128)(2,1)} %bitcast.19, f32[64,64]{1,0:T(8,128)} %vert_ref.1, f32[3]{0:T(128)} %latlen_ref.1, f32[3]{0:T(128)} %lonlen_ref.1, f32[3]{0:T(128)} %sw_ref.1, s32[1,8192]{1,0:T(1,128)} %bitcast.20, s32[1,8192]{1,0:T(1,128)} %bitcast.21, ...), custom_call_target="tpu_custom_call" | custom-call | tf_op jit(solution)/shard_map/pallas_call | solution.py:466
  168.7 0.0 copy-start
  168.7 2.5 %copy.13 = f32[1,64,6,768]{3,1,2,0:T(8,128)} copy(f32[1,64,6,768]{3,1,2,0:T(8,128)} %bitcast.18) | data formatting | bytes 2359296
  171.2 0.0 copy-done
  171.2 1.0 copy.14
Async XLA Ops:
  168.7 2.5 %copy-start = (f32[384,768]{1,0:T(8,128)S(1)}, f32[384,768]{1,0:T(8,128)}, u32[]{:S(2)}) copy-start(f32[384,768]{1,0:T(8,128)} %get-tuple-element.5) | copy-start | bytes 3538948

commit v6 on v5

--- a/solution.py
+++ b/solution.py
@@ -20,7 +20,6 @@
 WIDE = LEV * PAD
 SCALES = 3
 OBS = 8192
-BLOCK = 256
 EDGE = 128
 TILE = 128
 TILES = NX // TILE
@@ -33,7 +32,8 @@
 BF = jnp.bfloat16
 F32 = jnp.float32
 
-PP, S1, A1, B1, TT, RS, S2, A2, B2, RR, SM, SL, UU = range(13)
+PP, S1, A1, B1, TT, RS, S2, A2, B2, SM, SL, UU = range(12)
+RR = UU + 3
 
 
 def iota(shape, dim):
@@ -54,8 +54,10 @@
     accept_ref,
     innov_ref,
     prec_ref,
-    control_ref,
-    gradient_ref,
+    f_out,
+    h_out,
+    first_ref,
+    second_ref,
     perm,
     lat_tab,
     lon_tab,
@@ -65,7 +67,6 @@
     col_ref,
     spread,
     weight,
-    acc,
     across,
     flat,
     send_p,
@@ -93,6 +94,7 @@
     sums_lat,
     send_sem,
     recv_sem,
+    out_sem,
 ):
     z = lax.axis_index("lat_0")
     y = lax.axis_index("lat_1")
@@ -143,17 +145,23 @@
 
         lax.fori_loop(first, last, go, 0)
 
-    def group_start(src, dst, g):
+    def group_start(src, dst, phase):
+        def start(g):
+            cols = pl.ds(g * GROUP, GROUP)
+
+            def go(k, carry):
+                there, to = lat_peer(k)
+                here = src.at[there, pl.ds(0, ROWS), cols]
+                remote(here, dst.at[band, pl.ds(0, ROWS), cols], phase + g, to).start()
+                return carry
+
+            lax.fori_loop(0, BANDS - 1, go, 0)
+
+        return start
+
+    def group_bytes(ref, g, sem):
         cols = pl.ds(g * GROUP, GROUP)
-
-        def go(k, carry):
-            there, to = lat_peer(k)
-            remote(
-                src.at[there, pl.ds(0, ROWS), cols], dst.at[band, pl.ds(0, ROWS), cols], UU + g, to
-            ).start()
-            return carry
-
-        lax.fori_loop(0, BANDS - 1, go, 0)
+        wait_bytes(ref.at[pl.ds(0, BANDS - 1), pl.ds(0, ROWS), cols], sem)
 
     def wait_bytes(ref, sem):
         pltpu.make_async_copy(ref, ref, sem).wait()
@@ -186,7 +194,7 @@
             at_line = iota((LINES, CHUNK), 0) == line_ref[:, here]
             at_col = (iota((TILE, CHUNK), 0) == col_ref[:, here]).astype(F32).astype(BF)
             total = target[...]
-            for piece in (high, values - high):
+            for piece in (high,) if with_innovation else (high, values - high):
                 picked = jnp.where(at_line, piece, 0.0).astype(BF)
                 total = total + lax.dot_general(
                     picked, at_col, (((1,), (1,)), ((), ())), preferred_element_type=F32
@@ -238,21 +246,24 @@
             product = recv_p[:, :, cols].astype(F32) * every[t].astype(F32)
             flat[:, cols] = product.astype(BF).reshape(WIDE, TILE)
 
-    def correlate(target):
-        acc[...] = jnp.zeros((WIDE, NX), F32)
-
-        def scale(s, carry):
+    def correlate(target, then=None):
+        def lat(s, carry):
             rows = dot(lat_tab[s], flat[...]).astype(BF)
-            across[:, EDGE : EDGE + NX] = rows
-            across[:, :EDGE] = rows[:, NX - EDGE :]
-            across[:, EDGE + NX :] = rows[:, :EDGE]
-            for first in range(0, NX, BLOCK):
-                window = across[:, first : first + BLOCK + 2 * EDGE]
-                acc[:, first : first + BLOCK] += sw_ref[s] * dot(window, lon_tab[s])
+            across[s, :, EDGE : EDGE + NX] = rows
+            across[s, :, :EDGE] = rows[:, NX - EDGE :]
+            across[s, :, EDGE + NX :] = rows[:, :EDGE]
             return carry
 
-        lax.fori_loop(0, SCALES, scale, 0)
-        target[...] = acc[...].astype(BF).reshape(LEV, PAD, NX)
+        lax.fori_loop(0, SCALES, lat, 0)
+        for g in range(GROUPS):
+            first = g * GROUP
+            total = jnp.zeros((WIDE, GROUP), F32)
+            for s in range(SCALES):
+                window = across[s, :, first : first + GROUP + 2 * EDGE]
+                total = total + sw_ref[s] * dot(window, lon_tab[s])
+            target[:, :, first : first + GROUP] = total.astype(BF).reshape(LEV, PAD, GROUP)
+            if then is not None:
+                then(g)
 
     def mix(tables, source):
         flat[...] = source[...].reshape(WIDE, NX)
@@ -276,7 +287,7 @@
         lax.fori_loop(0, SCALES, lat, 0)
 
         def lon(s, carry):
-            tall = (BLOCK + 2 * EDGE, BLOCK)
+            tall = (GROUP + 2 * EDGE, GROUP)
             gap = iota(tall, 0) - EDGE - iota(tall, 1)
             scaled = gap.astype(F32) / lonlen_ref[s]
             lon_tab[s] = jnp.exp(-0.5 * scaled * scaled).astype(BF)
@@ -333,9 +344,7 @@
     correlate(send_t)
     lat_start(send_t, recv_t, TT, 0, EARLY)
     flat[...] = send_t[...].reshape(WIDE, NX)
-    correlate(send_u)
-    for g in range(GROUPS):
-        group_start(send_u, recv_u, g)
+    correlate(send_u, group_start(send_u, recv_u, UU))
     recv_u[band] = send_u[band]
     recv_t[band] = send_t[band]
 
@@ -352,7 +361,7 @@
 
     for g in range(GROUPS):
         cols = slice(g * GROUP, (g + 1) * GROUP)
-        wait_bytes(recv_u.at[pl.ds(0, BANDS - 1), pl.ds(0, ROWS), cols], recv_sem.at[UU + g])
+        group_bytes(recv_u, g, recv_sem.at[UU + g])
         got = recv_u[:, :, cols].reshape(WIDE, GROUP)
         mixed = dot(image_mix[0], got) + dot(image_mix[1], got)
         partial = (pert_ref[:, :, cols].astype(F32).reshape(LINES, GROUP) * mixed).astype(BF)
@@ -380,13 +389,19 @@
 
     tile_gather(tile_out_two, tile_in_two, tiles_two, S2, A2, B2)
     owner_schur(tiles_two)
-    correlate(send_r)
-    lat_start(send_r, recv_r, RR)
+    correlate(send_r, group_start(send_r, recv_r, RR))
     lat_start(send_t, recv_t, TT, TAIL, BANDS - 1)
     recv_r[band] = send_r[band]
-    lat_recv(recv_r, RR)
-    h_ref[...] = -mix(grad_mix, recv_r)
-    row = jnp.where(lane == 2, jnp.sum(h_ref[...] * h_ref[...]), stats[...])
+    hess_square = 0.0
+    for g in range(GROUPS):
+        cols = slice(g * GROUP, (g + 1) * GROUP)
+        group_bytes(recv_r, g, recv_sem.at[RR + g])
+        got = recv_r[:, :, cols].reshape(WIDE, GROUP)
+        hess = -(dot(grad_mix[0], got) + dot(grad_mix[1], got))
+        h_ref[:, cols] = hess
+        hess_square = hess_square + jnp.sum(hess * hess)
+    row = jnp.where(lane == 2, hess_square, stats[...])
+    keep_h = pltpu.make_async_copy(h_ref, h_out, out_sem.at[1])
     row_mem[...] = row
 
     def tell_mem(k, carry):
@@ -407,8 +422,11 @@
 
     lax.fori_loop(0, BANDS - 1, tell_lat, 0)
     sums_lat[band] = row
+    keep_h.start()
     lat_recv(recv_t, TT)
     f_ref[...] = mix(grad_mix, recv_t)
+    keep_f = pltpu.make_async_copy(f_ref, f_out, out_sem.at[0])
+    keep_f.start()
     wait_bytes(sums_lat.at[pl.ds(0, BANDS - 1)], recv_sem.at[SL])
     total = jnp.sum(sums_lat[...], axis=0)
     grad_square, obs_square, hess_square = (
@@ -416,15 +434,16 @@
     )
     first_step = grad_square / (grad_square + obs_square)
     second_step = (grad_square + obs_square) / (grad_square + 2.0 * obs_square + hess_square)
-    gradient = f_ref[...] - first_step * (f_ref[...] + h_ref[...])
-    gradient_ref[...] = gradient
-    control_ref[...] = -first_step * f_ref[...] - second_step * gradient
-
-    for buffer, phase in ((send_p, PP), (send_t, TT), (send_r, RR)):
+    first_ref[...] = jnp.full((PAD, NX), first_step, F32)
+    second_ref[...] = jnp.full((PAD, NX), second_step, F32)
+    keep_f.wait()
+    keep_h.wait()
+
+    for buffer, phase in ((send_p, PP), (send_t, TT)):
         lat_sent(buffer, phase)
     for g in range(GROUPS):
-        cols = slice(g * GROUP, (g + 1) * GROUP)
-        wait_bytes(send_u.at[pl.ds(0, BANDS - 1), pl.ds(0, ROWS), cols], send_sem.at[UU + g])
+        group_bytes(send_u, g, send_sem.at[UU + g])
+        group_bytes(send_r, g, send_sem.at[RR + g])
 
     @pl.when(mem < TILES)
     def _():
@@ -443,6 +462,13 @@
 
     wait_bytes(sums_mem.at[pl.ds(0, MEMS - 1)], send_sem.at[SM])
     wait_bytes(sums_lat.at[pl.ds(0, BANDS - 1)], send_sem.at[SL])
+
+
+def finish(f_ref, h_ref, first_ref, second_ref, control_ref, gradient_ref):
+    first_step, second_step = first_ref[0:1, :], second_ref[0:1, :]
+    gradient = f_ref[...] - first_step * (f_ref[...] + h_ref[...])
+    gradient_ref[...] = gradient
+    control_ref[...] = -first_step * f_ref[...] - second_step * gradient
 
 
 def local(
@@ -458,31 +484,33 @@
 ):
     vmem = pl.BlockSpec(memory_space=pltpu.VMEM)
     smem = pl.BlockSpec(memory_space=pltpu.SMEM)
+    hbm = pl.BlockSpec(memory_space=pl.ANY)
     slab = pltpu.VMEM((BANDS, PAD, NX), BF)
     lines = pltpu.VMEM((LINES, NX), F32)
     chunk = pltpu.VMEM((LINES, TILE), F32)
     level_tile = pltpu.VMEM((BANDS, PAD, TILE), BF)
     all_tiles = pltpu.VMEM((MEMS, BANDS, PAD, TILE), BF)
-    new_control, gradient = pl.pallas_call(
+    grad, hess, first_step, second_step = pl.pallas_call(
         kernel,
         out_shape=(
             jax.ShapeDtypeStruct((LINES, NX), F32),
             jax.ShapeDtypeStruct((LINES, NX), F32),
+            jax.ShapeDtypeStruct((PAD, NX), F32),
+            jax.ShapeDtypeStruct((PAD, NX), F32),
         ),
         in_specs=[vmem, vmem, smem, smem, smem, vmem, vmem, vmem, vmem],
-        out_specs=(vmem, vmem),
+        out_specs=(hbm, hbm, vmem, vmem),
         scratch_shapes=[
             pltpu.VMEM((WIDE, LINES), BF),
             pltpu.VMEM((SCALES, WIDE, WIDE), BF),
-            pltpu.VMEM((SCALES, BLOCK + 2 * EDGE, BLOCK), BF),
+            pltpu.VMEM((SCALES, GROUP + 2 * EDGE, GROUP), BF),
             pltpu.VMEM((2, LINES, WIDE), BF),
             pltpu.VMEM((2, LINES, WIDE), BF),
             pltpu.VMEM((1, OBS), jnp.int32),
             pltpu.VMEM((1, OBS), jnp.int32),
             chunk,
             chunk,
-            pltpu.VMEM((WIDE, NX), F32),
-            pltpu.VMEM((WIDE, NX + 2 * EDGE), BF),
+            pltpu.VMEM((SCALES, WIDE, NX + 2 * EDGE), BF),
             pltpu.VMEM((WIDE, NX), BF),
             slab,
             slab,
@@ -507,8 +535,9 @@
             pltpu.VMEM((1, 128), F32),
             pltpu.VMEM((MEMS, 1, 128), F32),
             pltpu.VMEM((BANDS, 1, 128), F32),
-            pltpu.SemaphoreType.DMA((12 + GROUPS,)),
-            pltpu.SemaphoreType.DMA((12 + GROUPS,)),
+            pltpu.SemaphoreType.DMA((11 + 2 * GROUPS,)),
+            pltpu.SemaphoreType.DMA((11 + 2 * GROUPS,)),
+            pltpu.SemaphoreType.DMA((2,)),
         ],
         compiler_params=pltpu.CompilerParams(
             collective_id=0, has_side_effects=True, vmem_limit_bytes=62 * 1024 * 1024
@@ -524,6 +553,19 @@
         innovation.reshape(1, OBS),
         obs_precision.reshape(1, OBS),
     )
+    block = pl.BlockSpec((2 * LEV, NX), lambda i: (i, 0))
+    whole = pl.BlockSpec((PAD, NX), lambda i: (0, 0))
+    new_control, gradient = pl.pallas_call(
+        finish,
+        out_shape=(
+            jax.ShapeDtypeStruct((LINES, NX), F32),
+            jax.ShapeDtypeStruct((LINES, NX), F32),
+        ),
+        grid=(LINES // (2 * LEV),),
+        in_specs=[block, block, whole, whole],
+        out_specs=(block, block),
+        compiler_params=pltpu.CompilerParams(vmem_limit_bytes=62 * 1024 * 1024),
+    )(grad, hess, first_step, second_step)
 
     def placed(field):
         return field.reshape(ROWS, LEV, NX).transpose(1, 0, 2)[None]

time: 172 us -> 169 us (0.983)
  local copies, waits for them, and re-layouts: 3.5 us -> 0 us
    pallas_call x1, Pallas kernels: 168 us -> 164 us  [local(): pl.pallas_call(kernel, out_shape=(jax.ShapeDtypeStruct((LINES, NX), F32),...]
    pallas_call x0 -> x1, Pallas kernels: none -> 3.87 us  [local(): pl.pallas_call(finish, out_shape=(jax.ShapeDtypeStruct((LINES, NX), F32),...]
    unnamed x4 -> x0, local copies, waits for them, and re-layouts: 3.5 us -> none
where the time goes in v6:
time: 169 us
  Pallas kernels  168 us (99%)
    pallas_call x1, Pallas kernels, local(): pl.pallas_call(kernel, out_shape=(jax.ShapeDtypeStruct((LINES, NX), F32),...  164 us
    pallas_call x1, Pallas kernels, local(): pl.pallas_call(finish, out_shape=(jax.ShapeDtypeStruct((LINES, NX), F32),...  3.87 us

profile of v6, /device:TPU:1, one launch (start us, length us, event | category | flops | bytes accessed | tf_op | source)
XLA Modules:
  0.0 168.7 jit_solution(16880972551898883803)
XLA Ops:
  0.6 164.1 %shard_map.104 = (f32[384,768]{1,0:T(8,128)}, f32[384,768]{1,0:T(8,128)}, f32[8,768]{1,0:T(8,128)}, f32[8,768]{1,0:T(8,128)}) custom-call(bf16[6,64,768]{2,1,0:T(8,128)(2,1)} %bitcast.17, f32[64,64]{1,0:T(8,128)} %vert_ref.1, f32[3]{0:T(128)} %latlen_ref.1, f32[3]{0:T(128)} %lonlen_ref.1, f32[3]{0:T(128)} %sw_ref.1, s32[1,8192]{1,0:T(1,128)} %bitcast.18, ...), custom_call_target="tpu_custom_call" | custom-call | tf_op jit(solution)/shard_map/pallas_call | solution.py:493
  164.8 3.9 %shard_map.105 = (f32[384,768]{1,0:T(8,128)}, f32[384,768]{1,0:T(8,128)}) custom-call(f32[384,768]{1,0:T(8,128)} %get-tuple-element.8.f_ref, f32[384,768]{1,0:T(8,128)} %get-tuple-element.9.h_ref, f32[8,768]{1,0:T(8,128)} %get-tuple-element.10.first_ref, f32[8,768]{1,0:T(8,128)} %get-tuple-element.11.second_ref), custom_call_target="tpu_custom_call" | custom-call | tf_op jit(solution)/shard_map/pallas_call | solution.py:558

commit v7 on v6

--- a/solution.py
+++ b/solution.py
@@ -25,9 +25,9 @@
 TILES = NX // TILE
 GROUP = 256
 GROUPS = NX // GROUP
-EARLY = 4
-NEAR = 8
-TAIL = 40
+EARLY = 2
+NEAR = 7
+TAIL = 37
 CHUNK = 512
 BF = jnp.bfloat16
 F32 = jnp.float32

time: 169 us -> 168 us (level)
  no operation moved by 1% of the time
where the time goes in v7:
time: 168 us
  Pallas kernels  167 us (99%)
    pallas_call x1, Pallas kernels, local(): pl.pallas_call(kernel, out_shape=(jax.ShapeDtypeStruct((LINES, NX), F32),...  163 us
    pallas_call x1, Pallas kernels, local(): pl.pallas_call(finish, out_shape=(jax.ShapeDtypeStruct((LINES, NX), F32),...  3.87 us

profile of v7, /device:TPU:1, one launch (start us, length us, event | category | flops | bytes accessed | tf_op | source)
XLA Modules:
  0.0 167.9 jit_solution(9198490099865467734)
XLA Ops:
  0.6 163.4 %shard_map.104 = (f32[384,768]{1,0:T(8,128)}, f32[384,768]{1,0:T(8,128)}, f32[8,768]{1,0:T(8,128)}, f32[8,768]{1,0:T(8,128)}) custom-call(bf16[6,64,768]{2,1,0:T(8,128)(2,1)} %bitcast.17, f32[64,64]{1,0:T(8,128)} %vert_ref.1, f32[3]{0:T(128)} %latlen_ref.1, f32[3]{0:T(128)} %lonlen_ref.1, f32[3]{0:T(128)} %sw_ref.1, s32[1,8192]{1,0:T(1,128)} %bitcast.18, ...), custom_call_target="tpu_custom_call" | custom-call | tf_op jit(solution)/shard_map/pallas_call | solution.py:493
  164.0 3.9 %shard_map.105 = (f32[384,768]{1,0:T(8,128)}, f32[384,768]{1,0:T(8,128)}) custom-call(f32[384,768]{1,0:T(8,128)} %get-tuple-element.8.f_ref, f32[384,768]{1,0:T(8,128)} %get-tuple-element.9.h_ref, f32[8,768]{1,0:T(8,128)} %get-tuple-element.10.first_ref, f32[8,768]{1,0:T(8,128)} %get-tuple-element.11.second_ref), custom_call_target="tpu_custom_call" | custom-call | tf_op jit(solution)/shard_map/pallas_call | solution.py:558
